TPU v7x, 1024 devices: a whole 8x8x8 slice. The times are simulated.
1024 devices in a mesh: group: 16 (over x, core), seq: 32 (over z_hi, y), tp: 2 (over z_lo).
Axes of the slice: x: 8, y: 8, z: 8 (z_hi: 4, z_lo: 2; z = z_hi * 2 + z_lo), core: 2. Of those that a mesh axis runs over, the one named last changes fastest.
Arguments:
- queries: bfloat16 [32, 2048, 4096], P('seq', 'group', 'tp'), may hold values from -256 to 256
- keys: bfloat16 [32, 2048, 512], P('seq', 'group', 'tp'), may hold values from -12 to 12
- values: bfloat16 [32, 2048, 512], P('seq', 'group', 'tp'), may hold values from -6 to 6
- moe_x: bfloat16 [16, 1024, 2048], P('group', ('seq', 'tp')), may hold values from -6 to 6
- expert_ids: int32 [16, 1024, 8], P('group', ('seq', 'tp')), may hold values from 0 to 63, all different within a row; in each aligned block of 16 rows (0 to 15, 16 to 31, ..., all dimensions but the last counted through in order) at most 3 rows name the same one
- gates: float32 [16, 1024, 8], P('group', ('seq', 'tp')), may hold values from 0.05 to 0.5
- grad_out: bfloat16 [16, 1024, 2048], P('group', ('seq', 'tp')), may hold values from -6 to 6
- w_gate: bfloat16 [64, 2048, 384], P(('seq', 'tp')), may hold values from -0.125 to 0.125
- w_up: bfloat16 [64, 2048, 384], P(('seq', 'tp')), may hold values from -0.125 to 0.125
- w_down: bfloat16 [64, 384, 2048], P(('seq', 'tp')), may hold values from -0.3125 to 0.3125
Outputs:
- attn_out: bfloat16 [32, 2048, 4096], P('seq', 'group', 'tp')
- moe_out: bfloat16 [16, 1024, 2048], P('group', ('seq', 'tp'))
- moe_grad_in: bfloat16 [16, 1024, 2048], P('group', ('seq', 'tp'))
Inputs may be any that keep to these rules, and one draw needn't show every extreme that they name: `expert_ids`: each token names 8 different experts. Within each aligned block of 16 tokens (the tokens of one device, in order), no expert is named by more than 3 tokens, and in every draw some block names some expert exactly 3 times.
All inputs are finite; a program needn't handle non-finite values.
Results may differ from a plain program's by a relative error of at most 0.0064.
Values may be sent and summed in bfloat16 or wider, within the bound.
A program may use at most 32 MiB of HBM per device.

v0:
```python
import jax
import jax.numpy as jnp
from jax import lax
from jax.sharding import PartitionSpec as P

H = 32
KVH = 4
HD = 128
EXPERTS = 64
CAP = 3


def for_sending(array):
    return jax.tree.map(lambda a: a.astype(jnp.bfloat16) if a.dtype == jnp.float32 else a, array)


def attend_head(query_rows, key_rows, value_rows):
    seq_len = query_rows.shape[0]
    block_len = min(512, seq_len)
    score_scale = 1.0 / query_rows.shape[1] ** 0.5
    pieces = []
    for first_row in range(0, seq_len, block_len):
        last_row = first_row + block_len
        scores = (
            lax.dot_general(
                query_rows[first_row:last_row],
                key_rows[:last_row],
                (((1,), (1,)), ((), ())),
                preferred_element_type=jnp.float32,
            )
            * score_scale
        )
        row_pos = first_row + lax.broadcasted_iota(jnp.int32, (block_len, last_row), 0)
        col_pos = lax.broadcasted_iota(jnp.int32, (block_len, last_row), 1)
        scores = jnp.where(col_pos <= row_pos, scores, -jnp.inf)
        row_max = jnp.max(scores, axis=1, keepdims=True)
        exp_scores = jnp.exp(scores - row_max)
        row_total = jnp.sum(exp_scores, axis=1, keepdims=True)
        mixed_rows = jnp.dot(
            exp_scores.astype(jnp.bfloat16),
            value_rows[:last_row],
            preferred_element_type=jnp.float32,
        )
        pieces.append((mixed_rows / row_total).astype(jnp.bfloat16))
    return jnp.concatenate(pieces, axis=0)


def route_tables(expert_ids, gates):
    route_ids = expert_ids[0]
    flat_ids = route_ids.reshape(-1)
    onehot = (
        flat_ids[:, None] == lax.broadcasted_iota(jnp.int32, (flat_ids.shape[0], EXPERTS), 1)
    ).astype(jnp.int32)
    before = jnp.cumsum(onehot, axis=0) - onehot
    slot_place = (flat_ids * CAP + jnp.sum(before * onehot, axis=1)).reshape(route_ids.shape)
    slot_match = slot_place[None, :, :] == lax.broadcasted_iota(
        jnp.int32, (EXPERTS * CAP, route_ids.shape[0], route_ids.shape[1]), 0
    )
    selector = jnp.sum(slot_match.astype(jnp.float32), axis=2)
    weighted = jnp.sum(jnp.where(slot_match, gates[0][None, :, :], 0.0), axis=2)
    return (selector, weighted)


def expert_math(token_rows, grad_rows, w_gate, w_up, w_down):
    hgate = jnp.einsum("secd,edf->secf", token_rows, w_gate, preferred_element_type=jnp.float32)
    hup = jnp.einsum("secd,edf->secf", token_rows, w_up, preferred_element_type=jnp.float32)
    sigmoid_gate = jax.nn.sigmoid(hgate)
    silu_gate = hgate * sigmoid_gate
    activated = (silu_gate * hup).astype(jnp.bfloat16)
    expert_out = jnp.einsum(
        "secf,efd->secd", activated, w_down, preferred_element_type=jnp.float32
    ).astype(jnp.bfloat16)
    grad_act = jnp.einsum("secd,efd->secf", grad_rows, w_down, preferred_element_type=jnp.float32)
    grad_gate = (grad_act * hup * sigmoid_gate * (1.0 + hgate * (1.0 - sigmoid_gate))).astype(
        jnp.bfloat16
    )
    grad_up = (grad_act * silu_gate).astype(jnp.bfloat16)
    input_grad = jnp.einsum("secf,edf->secd", grad_gate, w_gate, preferred_element_type=jnp.float32)
    input_grad = input_grad + jnp.einsum(
        "secf,edf->secd", grad_up, w_up, preferred_element_type=jnp.float32
    )
    return (expert_out, input_grad.astype(jnp.bfloat16))


def shards(queries, keys, values, moe_x, expert_ids, gates, grad_out, w_gate, w_up, w_down):
    tok_rows = queries.shape[1]
    group_count = lax.axis_size("group")
    tp_count = lax.axis_size("tp")
    local_queries = H // tp_count
    per_device = local_queries // group_count
    kv_local = KVH // tp_count
    repeats = group_count // kv_local
    query_heads = queries[0].reshape(tok_rows, group_count, per_device, HD)
    key_heads = jnp.broadcast_to(
        keys[0].reshape(tok_rows, kv_local, 1, HD), (tok_rows, kv_local, repeats, HD)
    ).reshape(tok_rows, group_count, 1, HD)
    value_heads = jnp.broadcast_to(
        values[0].reshape(tok_rows, kv_local, 1, HD), (tok_rows, kv_local, repeats, HD)
    ).reshape(tok_rows, group_count, 1, HD)
    head_queries, head_keys, head_values = (
        lax.all_to_all(query_heads, "group", split_axis=1, concat_axis=0, tiled=True),
        lax.all_to_all(key_heads, "group", split_axis=1, concat_axis=0, tiled=True),
        lax.all_to_all(value_heads, "group", split_axis=1, concat_axis=0, tiled=True),
    )
    attended = jax.vmap(attend_head, in_axes=(1, None, None), out_axes=1)(
        head_queries[:, 0], head_keys[:, 0, 0], head_values[:, 0, 0]
    )
    restored = lax.all_to_all(
        for_sending(attended[:, None]), "group", split_axis=0, concat_axis=1, tiled=True
    )
    attn_out = restored.reshape(1, tok_rows, local_queries * HD)
    selector, weighted = route_tables(expert_ids, gates)
    send_rows = jnp.dot(
        selector.astype(jnp.bfloat16), moe_x[0], preferred_element_type=jnp.float32
    ).astype(jnp.bfloat16)
    send_grads = jnp.dot(
        weighted, grad_out[0].astype(jnp.float32), precision=lax.Precision.HIGHEST
    ).astype(jnp.bfloat16)
    devices = lax.axis_size(("seq", "tp"))
    local_experts = EXPERTS // devices
    width = send_rows.shape[1]
    buffer_shape = (devices, local_experts, CAP, width)
    recv_rows, recv_grads = (
        lax.all_to_all(
            send_rows.reshape(buffer_shape), ("seq", "tp"), split_axis=0, concat_axis=0, tiled=True
        ),
        lax.all_to_all(
            send_grads.reshape(buffer_shape), ("seq", "tp"), split_axis=0, concat_axis=0, tiled=True
        ),
    )
    expert_out, input_grad = expert_math(recv_rows, recv_grads, w_gate, w_up, w_down)
    back_out, back_grad = (
        lax.all_to_all(expert_out, ("seq", "tp"), split_axis=0, concat_axis=0, tiled=True),
        lax.all_to_all(input_grad, ("seq", "tp"), split_axis=0, concat_axis=0, tiled=True),
    )
    slot_out = back_out.reshape(EXPERTS * CAP, width).astype(jnp.float32)
    slot_grad = back_grad.reshape(EXPERTS * CAP, width).astype(jnp.float32)
    moe_out = lax.dot_general(
        weighted, slot_out, (((0,), (0,)), ((), ())), precision=lax.Precision.HIGHEST
    )
    moe_grad_in = lax.dot_general(
        selector, slot_grad, (((0,), (0,)), ((), ())), precision=lax.Precision.HIGHEST
    )
    return (attn_out, moe_out.astype(jnp.bfloat16)[None], moe_grad_in.astype(jnp.bfloat16)[None])


def solution(mesh):
    placed = (
        P("seq", "group", "tp"),
        P("seq", "group", "tp"),
        P("seq", "group", "tp"),
        P("group", ("seq", "tp"), None),
        P("group", ("seq", "tp"), None),
        P("group", ("seq", "tp"), None),
        P("group", ("seq", "tp"), None),
        P(("seq", "tp"), None, None),
        P(("seq", "tp"), None, None),
        P(("seq", "tp"), None, None),
    )
    return jax.shard_map(
        shards,
        mesh=mesh,
        in_specs=placed,
        out_specs=(
            P("seq", "group", "tp"),
            P("group", ("seq", "tp"), None),
            P("group", ("seq", "tp"), None),
        ),
        check_vma=False,
    )
```

profile of v0, /device:TPU:1, one launch (start us, length us, event | category | flops | bytes accessed | tf_op | source)
XLA Modules:
  0.0 258.7 jit_solution(5648351992381993250)
XLA Ops:
  2.6 17.6 %all-to-all-start.1 = ((bf16[128,16,1,128]{3,0,2,1:T(8,128)(2,1)}), bf16[128,16,1,128]{3,0,2,1:T(8,128)(2,1)S(1)}, u32[]{:S(2)}, u32[]{:S(2)}) async-start(bf16[128,16,1,128]{3,0,2,1:T(8,128)(2,1)} %bitcast.5), calls=%async_computation.1 | async-start | bytes 1048576 | tf_op jit(solution)/shard_map/all_to_all | solution.py:102
  21.1 16.4 %all-to-all-done.1 = bf16[128,16,1,128]{3,0,2,1:T(8,128)(2,1)S(1)} async-done(((bf16[128,16,1,128]{3,0,2,1:T(8,128)(2,1)}), bf16[128,16,1,128]{3,0,2,1:T(8,128)(2,1)S(1)}, u32[]{:S(2)}, u32[]{:S(2)}) %all-to-all-start.1) | async-done | bytes 524320 | tf_op jit(solution)/shard_map/all_to_all | solution.py:102
  38.4 3.5 %all-to-all-start.2 = ((bf16[128,16,1,128]{3,0,2,1:T(8,128)(2,1)}), bf16[128,16,1,128]{3,0,2,1:T(8,128)(2,1)S(1)}, u32[]{:S(2)}, u32[]{:S(2)}) async-start(bf16[128,16,1,128]{3,0,2,1:T(8,128)(2,1)} %bitcast.9), calls=%async_computation.2 | async-start | bytes 1048576 | tf_op jit(solution)/shard_map/all_to_all | solution.py:103
  43.6 14.9 %all-to-all-done.2 = bf16[128,16,1,128]{3,0,2,1:T(8,128)(2,1)S(1)} async-done(((bf16[128,16,1,128]{3,0,2,1:T(8,128)(2,1)}), bf16[128,16,1,128]{3,0,2,1:T(8,128)(2,1)S(1)}, u32[]{:S(2)}, u32[]{:S(2)}) %all-to-all-start.2) | async-done | bytes 524320 | tf_op jit(solution)/shard_map/all_to_all | solution.py:103
  58.5 4.1 %all-to-all-start = ((bf16[128,16,1,128]{0,3,2,1:T(8,128)(2,1)}), bf16[128,16,1,128]{0,3,2,1:T(8,128)(2,1)}, u32[]{:S(2)}, u32[]{:S(2)}) async-start(bf16[128,16,1,128]{0,3,2,1:T(8,128)(2,1)} %bitcast.1), calls=%async_computation | async-start | bytes 1048576 | tf_op jit(solution)/shard_map/all_to_all | solution.py:101
  63.4 1.3 reshape.375
  64.7 1.7 convolution_convert_fusion
  66.3 1.3 reshape.382
  72.9 6.0 %all-to-all-done = bf16[128,16,1,128]{0,3,2,1:T(8,128)(2,1)} async-done(((bf16[128,16,1,128]{0,3,2,1:T(8,128)(2,1)}), bf16[128,16,1,128]{0,3,2,1:T(8,128)(2,1)}, u32[]{:S(2)}, u32[]{:S(2)}) %all-to-all-start) | async-done | bytes 524320 | tf_op jit(solution)/shard_map/all_to_all | solution.py:101
  78.9 14.2 %all-to-all-start.4 = ((bf16[64,1,3,2048]{3,2,1,0:T(4,128)(2,1)}), bf16[64,1,3,2048]{3,2,1,0:T(4,128)(2,1)}, u32[]{:S(2)}, u32[]{:S(2)}) async-start(bf16[64,1,3,2048]{3,2,1,0:T(4,128)(2,1)} %bitcast.35), calls=%async_computation.4 | async-start | bytes 2097152 | tf_op jit(solution)/shard_map/all_to_all | solution.py:124
  93.0 1.3 copy.125
  95.1 1.2 fusion.91
  100.9 21.6 %all-to-all-done.4 = bf16[64,1,3,2048]{3,2,1,0:T(4,128)(2,1)} async-done(((bf16[64,1,3,2048]{3,2,1,0:T(4,128)(2,1)}), bf16[64,1,3,2048]{3,2,1,0:T(4,128)(2,1)}, u32[]{:S(2)}, u32[]{:S(2)}) %all-to-all-start.4) | async-done | bytes 786464 | tf_op jit(solution)/shard_map/all_to_all | solution.py:124
  122.6 8.8 %all-to-all-start.6 = ((bf16[64,1,3,2048]{3,2,1,0:T(4,128)(2,1)}), bf16[64,1,3,2048]{3,2,1,0:T(4,128)(2,1)}, u32[]{:S(2)}, u32[]{:S(2)}) async-start(bf16[64,1,3,2048]{3,2,1,0:T(4,128)(2,1)} %bitcast.57), calls=%async_computation.6 | async-start | bytes 2097152 | tf_op jit(solution)/shard_map/all_to_all | solution.py:127
  131.5 1.6 fusion.55
  138.0 2.1 fusion.29
  140.2 19.5 %all-to-all-done.6 = bf16[64,1,3,2048]{3,2,1,0:T(4,128)(2,1)} async-done(((bf16[64,1,3,2048]{3,2,1,0:T(4,128)(2,1)}), bf16[64,1,3,2048]{3,2,1,0:T(4,128)(2,1)}, u32[]{:S(2)}, u32[]{:S(2)}) %all-to-all-start.6) | async-done | bytes 786464 | tf_op jit(solution)/shard_map/all_to_all | solution.py:127
  159.6 5.3 %all-to-all-start.3 = ((bf16[16,2,8192]{2,1,0:T(2,128)(2,1)}), bf16[16,2,8192]{2,1,0:T(2,128)(2,1)S(1)}, u32[]{:S(2)}, u32[]{:S(2)}) async-start(bf16[16,2,8192]{2,1,0:T(2,128)(2,1)} %reshape.390), calls=%async_computation.3 | async-start | bytes 1048576 | tf_op jit(solution)/shard_map/all_to_all | solution.py:108
  164.9 2.7 %fusion.32 = f32[64,1,3,384]{3,0,2,1:T(8,128)S(1)} fusion(bf16[1,2048,384]{2,1,0:T(8,128)(2,1)} %param.18, bf16[64,1,3,2048]{3,2,1,0:T(4,128)(2,1)} %all-to-all-done.4), kind=kOutput, calls=%fused_computation.44 | convolution fusion | flops 301989888 | bytes 2654208 | tf_op jit(solution)/shard_map/secd,edf->secf/dot_general | solution.py:66
  167.7 2.3 fusion.35
  172.1 1.7 copy.139
  173.8 8.4 %all-to-all-done.3 = bf16[16,2,8192]{2,1,0:T(2,128)(2,1)S(1)} async-done(((bf16[16,2,8192]{2,1,0:T(2,128)(2,1)}), bf16[16,2,8192]{2,1,0:T(2,128)(2,1)S(1)}, u32[]{:S(2)}, u32[]{:S(2)}) %all-to-all-start.3) | async-done | bytes 524320 | tf_op jit(solution)/shard_map/all_to_all | solution.py:108
  182.2 7.5 %all-to-all-start.7 = ((bf16[64,1,3,2048]{3,2,1,0:T(4,128)(2,1)}), bf16[64,1,3,2048]{3,2,1,0:T(4,128)(2,1)S(1)}, u32[]{:S(2)}, u32[]{:S(2)}) async-start(bf16[64,1,3,2048]{3,2,1,0:T(4,128)(2,1)} %copy.139), calls=%async_computation.7 | async-start | bytes 2097152 | tf_op jit(solution)/shard_map/all_to_all | solution.py:134
  189.7 2.1 fusion.6
  191.8 1.7 copy.136
  193.5 25.8 %all-to-all-done.7 = bf16[64,1,3,2048]{3,2,1,0:T(4,128)(2,1)S(1)} async-done(((bf16[64,1,3,2048]{3,2,1,0:T(4,128)(2,1)}), bf16[64,1,3,2048]{3,2,1,0:T(4,128)(2,1)S(1)}, u32[]{:S(2)}, u32[]{:S(2)}) %all-to-all-start.7) | async-done | bytes 786464 | tf_op jit(solution)/shard_map/all_to_all | solution.py:134
  219.3 7.9 %all-to-all-start.5 = ((bf16[64,1,3,2048]{3,2,1,0:T(4,128)(2,1)}), bf16[64,1,3,2048]{3,2,1,0:T(4,128)(2,1)}, u32[]{:S(2)}, u32[]{:S(2)}) async-start(bf16[64,1,3,2048]{3,2,1,0:T(4,128)(2,1)} %copy.136), calls=%async_computation.5 | async-start | bytes 2097152 | tf_op jit(solution)/shard_map/all_to_all | solution.py:133
  227.2 1.8 reshape.391
  229.0 1.3 copy.141
  231.3 2.0 copy.140
  235.1 20.1 %all-to-all-done.5 = bf16[64,1,3,2048]{3,2,1,0:T(4,128)(2,1)} async-done(((bf16[64,1,3,2048]{3,2,1,0:T(4,128)(2,1)}), bf16[64,1,3,2048]{3,2,1,0:T(4,128)(2,1)}, u32[]{:S(2)}, u32[]{:S(2)}) %all-to-all-start.5) | async-done | bytes 786464 | tf_op jit(solution)/shard_map/all_to_all | solution.py:133
  255.3 2.4 reshape.381
  (93 shorter events, 27.6 us)
Async XLA Ops:
  0.6 137.4 %copy-start = (bf16[1,2048,384]{2,1,0:T(8,128)(2,1)S(1)}, bf16[1,2048,384]{2,1,0:T(8,128)(2,1)}, u32[]{:S(2)}) copy-start(bf16[1,2048,384]{2,1,0:T(8,128)(2,1)} %param.17) | copy-start | bytes 4718596
  0.6 41.2 %copy-start.5 = (bf16[1,128,2048]{2,1,0:T(8,128)(2,1)S(1)}, bf16[1,128,2048]{2,1,0:T(8,128)(2,1)}, u32[]{:S(2)}) copy-start(bf16[1,128,2048]{2,1,0:T(8,128)(2,1)} %param.10) | copy-start | bytes 1572868
  2.6 40.3 %copy-start.14 = (s32[1,16,8]{1,2,0:T(8,128)S(1)}, s32[1,16,8]{1,2,0:T(8,128)}, u32[]{:S(2)}) copy-start(s32[1,16,8]{1,2,0:T(8,128)} %param.14) | copy-start | bytes 1540
  2.6 34.9 %all-to-all-start.1 = ((bf16[128,16,1,128]{3,0,2,1:T(8,128)(2,1)}), bf16[128,16,1,128]{3,0,2,1:T(8,128)(2,1)S(1)}, u32[]{:S(2)}, u32[]{:S(2)}) async-start(bf16[128,16,1,128]{3,0,2,1:T(8,128)(2,1)} %bitcast.5), calls=%async_computation.1 | async-start | bytes 1048576 | tf_op jit(solution)/shard_map/all_to_all | solution.py:102
  21.0 41.7 %copy-start.15 = (f32[1,16,8]{1,2,0:T(8,128)S(1)}, f32[1,16,8]{1,2,0:T(8,128)}, u32[]{:S(2)}) copy-start(f32[1,16,8]{1,2,0:T(8,128)} %param.15) | copy-start | bytes 1540
  21.1 41.9 %copy-start.13 = (bf16[1,16,2048]{2,1,0:T(8,128)(2,1)S(1)}, bf16[1,16,2048]{2,1,0:T(8,128)(2,1)}, u32[]{:S(2)}) copy-start(bf16[1,16,2048]{2,1,0:T(8,128)(2,1)} %param.13) | copy-start | bytes 196612
  38.4 20.1 %all-to-all-start.2 = ((bf16[128,16,1,128]{3,0,2,1:T(8,128)(2,1)}), bf16[128,16,1,128]{3,0,2,1:T(8,128)(2,1)S(1)}, u32[]{:S(2)}, u32[]{:S(2)}) async-start(bf16[128,16,1,128]{3,0,2,1:T(8,128)(2,1)} %bitcast.9), calls=%async_computation.2 | async-start | bytes 1048576 | tf_op jit(solution)/shard_map/all_to_all | solution.py:103
  58.5 20.4 %all-to-all-start = ((bf16[128,16,1,128]{0,3,2,1:T(8,128)(2,1)}), bf16[128,16,1,128]{0,3,2,1:T(8,128)(2,1)}, u32[]{:S(2)}, u32[]{:S(2)}) async-start(bf16[128,16,1,128]{0,3,2,1:T(8,128)(2,1)} %bitcast.1), calls=%async_computation | async-start | bytes 1048576 | tf_op jit(solution)/shard_map/all_to_all | solution.py:101
  63.0 4.6 %copy-start.9 = (f32[192,16]{0,1:T(8,128)}, f32[192,16]{0,1:T(8,128)S(1)}, u32[]{:S(2)}) copy-start(f32[192,16]{0,1:T(8,128)S(1)} %get-tuple-element.12) | copy-start | bytes 36868
  78.9 43.7 %all-to-all-start.4 = ((bf16[64,1,3,2048]{3,2,1,0:T(4,128)(2,1)}), bf16[64,1,3,2048]{3,2,1,0:T(4,128)(2,1)}, u32[]{:S(2)}, u32[]{:S(2)}) async-start(bf16[64,1,3,2048]{3,2,1,0:T(4,128)(2,1)} %bitcast.35), calls=%async_computation.4 | async-start | bytes 2097152 | tf_op jit(solution)/shard_map/all_to_all | solution.py:124
  94.3 2.9 %copy-start.8 = (bf16[8,128,1,1,128]{4,1,0,3,2:T(8,128)(2,1)S(1)}, bf16[8,128,1,1,128]{4,1,0,3,2:T(8,128)(2,1)}, u32[]{:S(2)}) copy-start(bf16[8,128,1,1,128]{4,1,0,3,2:T(8,128)(2,1)} %slice.72) | copy-start | bytes 786436
  94.4 2.9 %copy-start.21 = (s32[512]{0:T(512)S(1)}, s32[512]{0:T(512)}, u32[]{:S(2)}) copy-start(s32[512]{0:T(512)} %iota_add_fusion.2) | copy-start | bytes 6148
  96.3 1.0 copy-start.4
  96.3 1.0 copy-start.16
  97.3 1.1 copy-start.7
  97.8 1.0 copy-start.6
  97.9 1.0 copy-start.20
  100.2 31.2 %copy-start.11 = (bf16[4,128,1,1,128]{4,1,0,3,2:T(8,128)(2,1)S(1)}, bf16[4,128,1,1,128]{4,1,0,3,2:T(8,128)(2,1)}, u32[]{:S(2)}) copy-start(bf16[4,128,1,1,128]{4,1,0,3,2:T(8,128)(2,1)} %slice.70) | copy-start | bytes 393220
  100.9 30.5 %copy-start.17 = (f32[512]{0:T(512)S(1)}, f32[512]{0:T(512)}, u32[]{:S(2)}) copy-start(f32[512]{0:T(512)} %copy-done.16) | copy-start | bytes 6148
  100.9 30.5 %copy-start.18 = (f32[512]{0:T(512)S(1)}, f32[512]{0:T(512)}, u32[]{:S(2)}) copy-start(f32[512]{0:T(512)} %fusion.62) | copy-start | bytes 6148
  100.9 32.1 %copy-start.12 = (bf16[4,128,1,1,128]{4,1,0,3,2:T(8,128)(2,1)S(1)}, bf16[4,128,1,1,128]{4,1,0,3,2:T(8,128)(2,1)}, u32[]{:S(2)}) copy-start(bf16[4,128,1,1,128]{4,1,0,3,2:T(8,128)(2,1)} %get-tuple-element.15) | copy-start | bytes 393220
  100.9 32.1 %copy-start.19 = (s32[512]{0:T(512)S(1)}, s32[512]{0:T(512)}, u32[]{:S(2)}) copy-start(s32[512]{0:T(512)} %iota_add_fusion) | copy-start | bytes 6148
  122.6 37.1 %all-to-all-start.6 = ((bf16[64,1,3,2048]{3,2,1,0:T(4,128)(2,1)}), bf16[64,1,3,2048]{3,2,1,0:T(4,128)(2,1)}, u32[]{:S(2)}, u32[]{:S(2)}) async-start(bf16[64,1,3,2048]{3,2,1,0:T(4,128)(2,1)} %bitcast.57), calls=%async_computation.6 | async-start | bytes 2097152 | tf_op jit(solution)/shard_map/all_to_all | solution.py:127
  159.6 22.6 %all-to-all-start.3 = ((bf16[16,2,8192]{2,1,0:T(2,128)(2,1)}), bf16[16,2,8192]{2,1,0:T(2,128)(2,1)S(1)}, u32[]{:S(2)}, u32[]{:S(2)}) async-start(bf16[16,2,8192]{2,1,0:T(2,128)(2,1)} %reshape.390), calls=%async_computation.3 | async-start | bytes 1048576 | tf_op jit(solution)/shard_map/all_to_all | solution.py:108
  164.9 2.7 %copy-start.2 = (bf16[1,384,2048]{2,1,0:T(8,128)(2,1)S(1)}, bf16[1,384,2048]{2,1,0:T(8,128)(2,1)}, u32[]{:S(2)}) copy-start(bf16[1,384,2048]{2,1,0:T(8,128)(2,1)} %param.19) | copy-start | bytes 4718596
  167.7 2.3 copy-start.3
  170.0 1.4 copy-start.1
  182.2 37.1 %all-to-all-start.7 = ((bf16[64,1,3,2048]{3,2,1,0:T(4,128)(2,1)}), bf16[64,1,3,2048]{3,2,1,0:T(4,128)(2,1)S(1)}, u32[]{:S(2)}, u32[]{:S(2)}) async-start(bf16[64,1,3,2048]{3,2,1,0:T(4,128)(2,1)} %copy.139), calls=%async_computation.7 | async-start | bytes 2097152 | tf_op jit(solution)/shard_map/all_to_all | solution.py:134
  219.3 35.9 %all-to-all-start.5 = ((bf16[64,1,3,2048]{3,2,1,0:T(4,128)(2,1)}), bf16[64,1,3,2048]{3,2,1,0:T(4,128)(2,1)}, u32[]{:S(2)}, u32[]{:S(2)}) async-start(bf16[64,1,3,2048]{3,2,1,0:T(4,128)(2,1)} %copy.136), calls=%async_computation.5 | async-start | bytes 2097152 | tf_op jit(solution)/shard_map/all_to_all | solution.py:133
  230.3 3.8 %copy-start.10 = (f32[192,16]{0,1:T(8,128)S(1)}, f32[192,16]{0,1:T(8,128)}, u32[]{:S(2)}) copy-start(f32[192,16]{0,1:T(8,128)} %copy-done.9) | copy-start | bytes 36868
where the time goes:
time: 260 us; the launch traced here: 259 us
  waiting for transfers between devices  133 us (51%)
  starting transfers between devices  68.8 us (26%)
  local copies, waits for them, and re-layouts  28.1 us (11%)
  matrix products  21.9 us (8%)
  other arithmetic  6.08 us (2%)
    all_to_all x1, waiting for transfers between devices, shards(): lax.all_to_all(input_grad, ('seq', 'tp'), split_axis=0, concat_axis=0, ti...  25.8 us
    all_to_all x1, waiting for transfers between devices, shards(): lax.all_to_all(send_rows.reshape(buffer_shape), ('seq', 'tp'), split_axis...  21.6 us
    all_to_all x1, waiting for transfers between devices, shards(): lax.all_to_all(expert_out, ('seq', 'tp'), split_axis=0, concat_axis=0, ti...  20.1 us
    all_to_all x1, waiting for transfers between devices, shards(): lax.all_to_all(send_grads.reshape(buffer_shape), ('seq', 'tp'), split_axi...  19.5 us
    all_to_all x1, starting transfers between devices, shards(): lax.all_to_all(key_heads, 'group', split_axis=1, concat_axis=0, tiled=True)  17.6 us
    all_to_all x1, waiting for transfers between devices, shards(): lax.all_to_all(key_heads, 'group', split_axis=1, concat_axis=0, tiled=True)  16.4 us
    all_to_all x1, waiting for transfers between devices, shards(): lax.all_to_all(value_heads, 'group', split_axis=1, concat_axis=0, tiled=T...  14.9 us
    all_to_all x1, starting transfers between devices, shards(): lax.all_to_all(send_rows.reshape(buffer_shape), ('seq', 'tp'), split_axis...  14.2 us
  transfers between devices with their start and end apart: 8, of which 8 were waited for; matrix products, arithmetic and copies ran while one was open for 19% of the time, Pallas kernels for 0%

commit v1 on v0

v1 whole, which is shorter than its diff:
```python
import functools

import jax
import jax.numpy as jnp
from jax import lax
from jax.experimental import pallas as pl
from jax.experimental.pallas import tpu as pltpu
from jax.sharding import PartitionSpec as P

H = 32
KVH = 4
HD = 128
CAP = 3
LINE = 8
CHUNK = 4
MESH = pl.DeviceIdType.MESH
NT_DIMS = (((1,), (1,)), ((), ()))
F32 = jnp.float32
BF16 = jnp.bfloat16
NEG = -1e30


def fused(
    cfg,
    x_ref,
    ids_ref,
    gates_ref,
    grad_ref,
    k_ref,
    v_ref,
    q_hbm,
    wg_hbm,
    wu_hbm,
    wd_hbm,
    attn_hbm,
    mo_ref,
    mg_ref,
    wg,
    wu,
    wd,
    qbuf,
    kbuf,
    vbuf,
    obuf,
    m_s,
    l_s,
    acc_s,
    meta,
    metag,
    xg,
    gg,
    sel_s,
    selg_s,
    sx,
    sg,
    rx,
    rg,
    so,
    si,
    bo,
    bi,
    po_s,
    pi_s,
    po,
    pi,
    line_send,
    line_recv,
    kv_send,
    kv_recv,
    pair_send,
    pair_recv,
    local_sem,
):
    n_group, line, tok, topk, chunk = cfg
    chips = n_group // 2
    rows = line * CAP * line
    part = CAP * line
    width = x_ref.shape[1]
    g = lax.axis_index("group")
    seq = lax.axis_index("seq")
    tp = lax.axis_index("tp")
    core = lax.rem(g, 2)
    chip = g // 2
    y = lax.rem(seq, line)
    z = (seq // line) * 2 + tp
    a = z + core * (y - z)
    b = y + core * (z - y)

    def peer(aa, bb):
        yy = bb + core * (aa - bb)
        zz = aa + core * (bb - aa)
        return (g, (zz // 2) * line + yy, lax.rem(zz, 2))

    def in_group(j):
        return (j, seq, tp)

    other = 1 - core
    sibling = in_group(2 * chip + other)

    loads = [
        pltpu.make_async_copy(wg_hbm, wg, local_sem.at[0]),
        pltpu.make_async_copy(wu_hbm, wu, local_sem.at[1]),
        pltpu.make_async_copy(wd_hbm, wd, local_sem.at[2]),
    ]
    for load in loads:
        load.start()
    half = qbuf.shape[2]
    mine = pl.ds(pl.multiple_of(core * half, half), half)
    theirs = pl.ds(pl.multiple_of(other * half, half), half)
    q_load = pltpu.make_async_copy(q_hbm.at[:, mine], qbuf.at[core], local_sem.at[3])
    q_load.start()

    barrier = pltpu.get_barrier_semaphore()

    def greet_line(i, carry):
        pl.semaphore_signal(barrier, 1, device_id=peer(lax.rem(a + i, line), b), device_id_type=MESH)
        pl.semaphore_signal(barrier, 1, device_id=peer(a, lax.rem(b + i, line)), device_id_type=MESH)
        return carry

    lax.fori_loop(1, line, greet_line, 0)

    def greet_group(i, carry):
        pl.semaphore_signal(
            barrier, 1, device_id=in_group(lax.rem(g + i, n_group)), device_id_type=MESH
        )
        return carry

    lax.fori_loop(1, n_group, greet_group, 0)

    meta[...] = jnp.zeros_like(meta)
    meta[0:tok, 0:topk] = ids_ref[...].astype(F32)
    meta[tok : 2 * tok, 0:topk] = gates_ref[...]
    metag[a] = meta[...]
    xg[a] = x_ref[...]
    gg[a] = grad_ref[...]
    head_k = pl.ds(pl.multiple_of(core * HD, HD), HD)
    kbuf[g] = k_ref[:, head_k]
    vbuf[g] = v_ref[:, head_k]

    @pl.when(lax.rem(chip, 2) == 0)
    def _():
        for extra in (2, 3):
            kbuf[2 * chip + extra] = jnp.zeros(kbuf.shape[1:], BF16)
            vbuf[2 * chip + extra] = jnp.zeros(vbuf.shape[1:], BF16)

    pl.semaphore_wait(barrier, 2 * (line - 1) + n_group - 1)

    def along_a(f, source, dest, i):
        p = lax.rem(a + i, line)
        return pltpu.make_async_remote_copy(
            src_ref=source(p),
            dst_ref=dest.at[a],
            send_sem=line_send.at[f, i],
            recv_sem=line_recv.at[f, a],
            device_id=peer(p, b),
            device_id_type=MESH,
        )

    def along_b(f, source, dest, i):
        p = lax.rem(b + i, line)
        return pltpu.make_async_remote_copy(
            src_ref=source(p),
            dst_ref=dest.at[b],
            send_sem=line_send.at[f, i],
            recv_sem=line_recv.at[f, b],
            device_id=peer(a, p),
            device_id_type=MESH,
        )

    def send_all(copy, f, source, dest):
        def step(i, carry):
            copy(f, source, dest, i).start()
            return carry

        lax.fori_loop(1, line, step, 0)

    def sent_all(copy, f, source, dest):
        def step(i, carry):
            copy(f, source, dest, i).wait_send()
            return carry

        lax.fori_loop(1, line, step, 0)

    def wait_all(f, me, dest):
        def step(i, carry):
            p = lax.rem(me + i, line)
            pltpu.make_async_remote_copy(
                src_ref=dest.at[p],
                dst_ref=dest.at[p],
                send_sem=line_send.at[f, i],
                recv_sem=line_recv.at[f, p],
                device_id=peer(a, b),
                device_id_type=MESH,
            ).wait_recv()
            return carry

        lax.fori_loop(1, line, step, 0)

    send_all(along_a, 0, lambda p: meta, metag)
    send_all(along_a, 1, lambda p: x_ref, xg)

    def kv_copy(j, what, source, dest):
        cols = pl.ds(pl.multiple_of(lax.rem(j, 2) * HD, HD), HD)
        return pltpu.make_async_remote_copy(
            src_ref=source.at[:, cols],
            dst_ref=dest.at[g],
            send_sem=kv_send.at[what, j],
            recv_sem=kv_recv.at[what, g],
            device_id=in_group(j),
            device_id_type=MESH,
        )

    def kv_start(j, carry):
        @pl.when(j != g)
        def _():
            kv_copy(j, 0, k_ref, kbuf).start()
            kv_copy(j, 1, v_ref, vbuf).start()

        return carry

    lax.fori_loop(2 * chip, n_group, kv_start, 0)
    q_send = pltpu.make_async_remote_copy(
        src_ref=q_hbm.at[:, theirs],
        dst_ref=qbuf.at[core],
        send_sem=pair_send.at[0],
        recv_sem=pair_recv.at[0],
        device_id=sibling,
        device_id_type=MESH,
    )
    q_send.start()
    send_all(along_a, 2, lambda p: grad_ref, gg)

    wait_all(0, a, metag)
    n_tok = line * tok
    lanes = meta.shape[1]
    ids_t = metag[:, 0:tok, :].reshape(n_tok, lanes).T[0:topk]
    gates_t = metag[:, tok : 2 * tok, :].reshape(n_tok, lanes).T[0:topk]
    place = lax.broadcasted_iota(jnp.int32, (line, n_tok), 0)
    first = ((a // 2) * line + place) * 2 + lax.rem(a, 2)
    second = ((place // 2) * line + a) * 2 + lax.rem(place, 2)
    expert = (first + core * (second - first)).astype(F32)
    named = jnp.zeros((line, n_tok), F32)
    gate = jnp.zeros((line, n_tok), F32)
    for k in range(topk):
        hit = jnp.where(ids_t[k : k + 1] == expert, 1.0, 0.0)
        named = named + hit
        gate = gate + hit * gates_t[k : k + 1]
    t_row = lax.broadcasted_iota(jnp.int32, (n_tok, n_tok), 0)
    t_col = lax.broadcasted_iota(jnp.int32, (n_tok, n_tok), 1)
    earlier = jnp.where((t_row // tok == t_col // tok) & (t_row < t_col), 1.0, 0.0)
    rank = jnp.dot(named.astype(BF16), earlier.astype(BF16), preferred_element_type=F32)
    own_block = jnp.where(place == lax.broadcasted_iota(jnp.int32, (line, n_tok), 1) // tok, 1.0, 0.0)
    for s in range(CAP):
        slot = jnp.where(rank == s, named, 0.0)
        slot_gate = slot * gate
        for d in range(line):
            at = pl.ds(d * part + s * line, line)
            sel_s[at] = own_block * slot[d : d + 1]
            selg_s[at] = own_block * slot_gate[d : d + 1]
    sel = sel_s[...]
    sel_b = sel.astype(BF16)
    gate_col = jnp.sum(selg_s[...], axis=1, keepdims=True)

    tile = min(width, 512)

    def rows_of(ref, cols):
        return jnp.concatenate(
            [ref[d, s, :, cols].astype(F32) for d in range(line) for s in range(CAP)], axis=0
        ).astype(BF16)

    def put_rows(ref, cols, value):
        for d in range(line):
            for s in range(CAP):
                r = d * part + s * line
                ref[d, s, :, cols] = value[r : r + line].astype(BF16)

    def pick(source, dest, received, scale):
        for c in range(0, width, tile):
            cols = slice(c, c + tile)
            block = source[:, :, cols].reshape(n_tok, tile)
            picked = jnp.dot(sel_b, block, preferred_element_type=F32)
            if scale is not None:
                picked = picked * scale
            put_rows(dest, cols, picked)
        received[b] = dest[b]

    wait_all(1, a, xg)
    pick(xg, sx, rx, None)
    send_all(along_b, 3, lambda p: sx.at[p], rx)
    wait_all(2, a, gg)
    pick(gg, sg, rg, gate_col)
    send_all(along_b, 4, lambda p: sg.at[p], rg)

    for load in loads:
        load.wait()

    wait_all(3, b, rx)
    ffe = wg.shape[1]
    hgate = jnp.zeros((rows, ffe), F32)
    hup = jnp.zeros((rows, ffe), F32)
    for c in range(0, width, tile):
        cols = slice(c, c + tile)
        token_rows = rows_of(rx, cols)
        hgate = hgate + jnp.dot(token_rows, wg[cols, :], preferred_element_type=F32)
        hup = hup + jnp.dot(token_rows, wu[cols, :], preferred_element_type=F32)
    sig = 1.0 / (1.0 + jnp.exp(-hgate))
    silu = hgate * sig
    act = (silu * hup).astype(BF16)
    for c in range(0, width, tile):
        cols = slice(c, c + tile)
        put_rows(so, cols, jnp.dot(act, wd[:, cols], preferred_element_type=F32))
    bo[b] = so[b]
    send_all(along_b, 5, lambda p: so.at[p], bo)

    wait_all(4, b, rg)
    grad_act = jnp.zeros((rows, ffe), F32)
    for c in range(0, width, tile):
        cols = slice(c, c + tile)
        grad_act = grad_act + lax.dot_general(
            rows_of(rg, cols), wd[:, cols], NT_DIMS, preferred_element_type=F32
        )
    grad_gate = (grad_act * hup * sig * (1.0 + hgate * (1.0 - sig))).astype(BF16)
    grad_up = (grad_act * silu).astype(BF16)
    for c in range(0, width, tile):
        cols = slice(c, c + tile)
        put_rows(
            si,
            cols,
            lax.dot_general(grad_gate, wg[cols, :], NT_DIMS, preferred_element_type=F32)
            + lax.dot_general(grad_up, wu[cols, :], NT_DIMS, preferred_element_type=F32),
        )
    bi[b] = si[b]
    send_all(along_b, 6, lambda p: si.at[p], bi)

    q_load.wait()
    q_send.wait_recv()

    def kv_wait(j, carry):
        @pl.when(j != g)
        def _():
            for what, dest in ((0, kbuf), (1, vbuf)):
                pltpu.make_async_remote_copy(
                    src_ref=dest.at[j],
                    dst_ref=dest.at[j],
                    send_sem=kv_send.at[what, j],
                    recv_sem=kv_recv.at[what, j],
                    device_id=sibling,
                    device_id_type=MESH,
                ).wait_recv()

        return carry

    lax.fori_loop(0, 2 * chip + 2, kv_wait, 0)
    n_heads = half // HD
    pos = k_ref.shape[0]
    q_rows = 2 * pos
    keys = chunk * pos
    m_s[...] = jnp.full_like(m_s, NEG)
    l_s[...] = jnp.zeros_like(l_s)
    acc_s[...] = jnp.zeros_like(acc_s)
    exp_scale = 1.4426950408889634 / HD**0.5

    def attend(j, carry):
        key_rows = kbuf[pl.ds(j * chunk, chunk)].reshape(keys, HD)
        value_rows = vbuf[pl.ds(j * chunk, chunk)].reshape(keys, HD)
        ahead = lax.broadcasted_iota(jnp.int32, (q_rows, keys), 1) - lax.broadcasted_iota(
            jnp.int32, (q_rows, keys), 0
        )
        seen = ahead <= q_rows * chip - keys * j
        for h in range(n_heads):
            cols = slice(h * HD, (h + 1) * HD)
            query_rows = qbuf[:, :, cols].reshape(q_rows, HD)
            scores = lax.dot_general(query_rows, key_rows, NT_DIMS, preferred_element_type=F32)
            scores = jnp.where(seen, scores, NEG)
            m_old = m_s[h]
            m_new = jnp.maximum(m_old, jnp.max(scores, axis=1, keepdims=True))
            alpha = jnp.exp2((m_old - m_new) * exp_scale)
            total = alpha * l_s[h]
            weights = []
            for c in range(0, keys, HD):
                e = jnp.exp2((scores[:, c : c + HD] - m_new) * exp_scale)
                total = total + e
                weights.append(e.astype(BF16))
            m_s[h] = m_new
            l_s[h] = total
            acc_s[h] = alpha * acc_s[h] + jnp.dot(
                jnp.concatenate(weights, axis=1), value_rows, preferred_element_type=F32
            )
        return carry

    lax.fori_loop(0, (2 * chip + 1 + chunk) // chunk, attend, 0)
    for h in range(n_heads):
        cols = slice(h * HD, (h + 1) * HD)
        done = acc_s[h] / jnp.sum(l_s[h], axis=1, keepdims=True)
        obuf[:, :, cols] = done.astype(BF16).reshape(2, pos, HD)
    o_send = pltpu.make_async_remote_copy(
        src_ref=obuf.at[other],
        dst_ref=attn_hbm.at[:, mine],
        send_sem=pair_send.at[1],
        recv_sem=pair_recv.at[1],
        device_id=sibling,
        device_id_type=MESH,
    )
    o_send.start()
    o_store = pltpu.make_async_copy(obuf.at[core], attn_hbm.at[:, mine], local_sem.at[3])
    o_store.start()

    gated_hi = selg_s[...].astype(BF16)
    gated_lo = (selg_s[...] - gated_hi.astype(F32)).astype(BF16)
    hi_t = gated_hi.astype(F32).T.astype(BF16)
    lo_t = gated_lo.astype(F32).T.astype(BF16)
    sel_t = sel.T.astype(BF16)

    def mix(returned, dest, final, lefts):
        for c in range(0, width, tile):
            cols = slice(c, c + tile)
            block = rows_of(returned, cols)
            mixed = jnp.dot(lefts[0], block, preferred_element_type=F32)
            for left in lefts[1:]:
                mixed = mixed + jnp.dot(left, block, preferred_element_type=F32)
            dest[:, :, cols] = mixed.astype(BF16).reshape(line, tok, tile)
        final[a] = dest[a]

    wait_all(5, b, bo)
    mix(bo, po_s, po, (hi_t, lo_t))
    send_all(along_a, 7, lambda p: po_s.at[p], po)
    wait_all(6, b, bi)
    mix(bi, pi_s, pi, (sel_t,))
    send_all(along_a, 8, lambda p: pi_s.at[p], pi)

    def add_up(final, out):
        total = final[0].astype(F32)
        for p in range(1, line):
            total = total + final[p].astype(F32)
        out[...] = total.astype(BF16)

    wait_all(7, a, po)
    add_up(po, mo_ref)
    wait_all(8, a, pi)
    add_up(pi, mg_ref)

    o_store.wait()
    o_send.wait()
    q_send.wait_send()
    sent_all(along_a, 0, lambda p: meta, metag)
    sent_all(along_a, 1, lambda p: x_ref, xg)
    sent_all(along_a, 2, lambda p: grad_ref, gg)
    sent_all(along_b, 3, lambda p: sx.at[p], rx)
    sent_all(along_b, 4, lambda p: sg.at[p], rg)
    sent_all(along_b, 5, lambda p: so.at[p], bo)
    sent_all(along_b, 6, lambda p: si.at[p], bi)
    sent_all(along_a, 7, lambda p: po_s.at[p], po)
    sent_all(along_a, 8, lambda p: pi_s.at[p], pi)

    def kv_sent(j, carry):
        @pl.when(j != g)
        def _():
            kv_copy(j, 0, k_ref, kbuf).wait_send()
            kv_copy(j, 1, v_ref, vbuf).wait_send()

        return carry

    lax.fori_loop(2 * chip, n_group, kv_sent, 0)


def shards(queries, keys, values, moe_x, expert_ids, gates, grad_out, w_gate, w_up, w_down):
    n_group = lax.axis_size("group")
    line = LINE
    pos, q_width = queries.shape[1:]
    tok, width = moe_x.shape[1:]
    topk = expert_ids.shape[2]
    ffe = w_gate.shape[2]
    half = q_width // 2
    n_heads = half // HD
    rows = line * CAP * line
    n_tok = line * tok
    chunk = min(CHUNK, n_group)
    vmem = pl.BlockSpec(memory_space=pltpu.VMEM)
    hbm = pl.BlockSpec(memory_space=pl.ANY)
    slots = pltpu.VMEM((line, CAP, line, width), BF16)
    block = pltpu.VMEM((line, tok, width), BF16)
    state = pltpu.VMEM((n_heads, 2 * pos, HD), F32)
    attn, out, grad_in = pl.pallas_call(
        functools.partial(fused, (n_group, line, tok, topk, chunk)),
        out_shape=(
            jax.ShapeDtypeStruct((pos, q_width), BF16),
            jax.ShapeDtypeStruct((tok, width), BF16),
            jax.ShapeDtypeStruct((tok, width), BF16),
        ),
        in_specs=[vmem] * 6 + [hbm] * 4,
        out_specs=(hbm, vmem, vmem),
        scratch_shapes=[
            pltpu.VMEM((width, ffe), BF16),
            pltpu.VMEM((width, ffe), BF16),
            pltpu.VMEM((ffe, width), BF16),
            pltpu.VMEM((2, pos, half), BF16),
            pltpu.VMEM((n_group, pos, HD), BF16),
            pltpu.VMEM((n_group, pos, HD), BF16),
            pltpu.VMEM((2, pos, half), BF16),
            state,
            state,
            state,
            pltpu.VMEM((2 * tok, 128), F32),
            pltpu.VMEM((line, 2 * tok, 128), F32),
            block,
            block,
            pltpu.VMEM((rows, n_tok), F32),
            pltpu.VMEM((rows, n_tok), F32),
        ]
        + [slots] * 8
        + [block] * 4
        + [
            pltpu.SemaphoreType.DMA((9, line)),
            pltpu.SemaphoreType.DMA((9, line)),
            pltpu.SemaphoreType.DMA((2, n_group)),
            pltpu.SemaphoreType.DMA((2, n_group)),
            pltpu.SemaphoreType.DMA((2,)),
            pltpu.SemaphoreType.DMA((2,)),
            pltpu.SemaphoreType.DMA((4,)),
        ],
        compiler_params=pltpu.CompilerParams(
            collective_id=0, has_side_effects=True, vmem_limit_bytes=60 * 1024 * 1024
        ),
    )(
        moe_x[0],
        expert_ids[0],
        gates[0],
        grad_out[0],
        keys[0],
        values[0],
        queries[0],
        w_gate[0],
        w_up[0],
        w_down[0],
    )
    return attn[None], out[None], grad_in[None]


def solution(mesh):
    tokens = P("group", ("seq", "tp"), None)
    heads = P("seq", "group", "tp")
    weights = P(("seq", "tp"), None, None)
    return jax.shard_map(
        shards,
        mesh=mesh,
        in_specs=(heads,) * 3 + (tokens,) * 4 + (weights,) * 3,
        out_specs=(heads, tokens, tokens),
        check_vma=False,
    )
```

time: 260 us -> 101 us (0.39)
  the two profiles are of different devices: /device:TPU:1 before, /device:TPU:10 now
where the time goes in v1:
time: 101 us
  Pallas kernels  92.7 us (92%)
  local copies, waits for them, and re-layouts  7.54 us (7%)
    pallas_call x1, Pallas kernels, shards(): pl.pallas_call(functools.partial(fused, (n_group, line, tok, topk, chunk)...  92.7 us
    unnamed x3, local copies, waits for them, and re-layouts  4.83 us

profile of v1, /device:TPU:10, one launch (start us, length us, event | category | flops | bytes accessed | tf_op | source)
XLA Modules:
  0.0 100.9 jit_solution(17462657216226952809)
XLA Ops:
  0.6 1.4 %copy.13.ids_ref = s32[16,8]{1,0:T(8,128)} copy(s32[16,8]{0,1:T(8,128)} %bitcast.24) | data formatting | bytes 1024 | tf_op jit(solution)/shard_map/squeeze | solution.py:526
  2.0 1.4 %copy.14.gates_ref = f32[16,8]{1,0:T(8,128)} copy(f32[16,8]{0,1:T(8,128)} %bitcast.25) | data formatting | bytes 1024 | tf_op jit(solution)/shard_map/squeeze | solution.py:527
  3.3 92.7 %shard_map.121 = (bf16[128,2048]{1,0:T(8,128)(2,1)}, bf16[16,2048]{1,0:T(8,128)(2,1)}, bf16[16,2048]{1,0:T(8,128)(2,1)}) custom-call(bf16[16,2048]{1,0:T(8,128)(2,1)} %bitcast.18, s32[16,8]{1,0:T(8,128)} %copy.13.ids_ref, f32[16,8]{1,0:T(8,128)} %copy.14.gates_ref, bf16[16,2048]{1,0:T(8,128)(2,1)} %bitcast.19, bf16[128,256]{1,0:T(8,128)(2,1)} %bitcast.20, ...), custom_call_target="tpu_custom_call" | custom-call | tf_op jit(solution)/shard_map/pallas_call | solution.py:483
  96.1 1.9 %copy.18 = bf16[1,128,2048]{2,1,0:T(8,128)(2,1)} copy(bf16[1,128,2048]{2,1,0:T(8,128)(2,1)} %bitcast.16) | data formatting | bytes 1048576
  98.0 1.5 %copy.19 = bf16[1,16,2048]{2,1,0:T(8,128)(2,1)} copy(bf16[1,16,2048]{2,1,0:T(8,128)(2,1)} %bitcast.23) | data formatting | bytes 131072
  99.4 1.5 %copy.20 = bf16[1,16,2048]{2,1,0:T(8,128)(2,1)} copy(bf16[1,16,2048]{2,1,0:T(8,128)(2,1)} %bitcast.22) | data formatting | bytes 131072

commit v2 on v1

--- a/solution.py
+++ b/solution.py
@@ -22,12 +22,12 @@
 
 def fused(
     cfg,
-    x_ref,
-    ids_ref,
-    gates_ref,
-    grad_ref,
-    k_ref,
-    v_ref,
+    x_hbm,
+    ids_hbm,
+    gates_hbm,
+    grad_hbm,
+    k_hbm,
+    v_hbm,
     q_hbm,
     wg_hbm,
     wu_hbm,
@@ -45,8 +45,8 @@
     m_s,
     l_s,
     acc_s,
-    meta,
-    metag,
+    idsg,
+    gatesg,
     xg,
     gg,
     sel_s,
@@ -61,7 +61,7 @@
     bi,
     po_s,
     pi_s,
-    po,
+    po_r,
     pi,
     line_send,
     line_recv,
@@ -75,7 +75,7 @@
     chips = n_group // 2
     rows = line * CAP * line
     part = CAP * line
-    width = x_ref.shape[1]
+    width = x_hbm.shape[1]
     g = lax.axis_index("group")
     seq = lax.axis_index("seq")
     tp = lax.axis_index("tp")
@@ -97,19 +97,6 @@
     other = 1 - core
     sibling = in_group(2 * chip + other)
 
-    loads = [
-        pltpu.make_async_copy(wg_hbm, wg, local_sem.at[0]),
-        pltpu.make_async_copy(wu_hbm, wu, local_sem.at[1]),
-        pltpu.make_async_copy(wd_hbm, wd, local_sem.at[2]),
-    ]
-    for load in loads:
-        load.start()
-    half = qbuf.shape[2]
-    mine = pl.ds(pl.multiple_of(core * half, half), half)
-    theirs = pl.ds(pl.multiple_of(other * half, half), half)
-    q_load = pltpu.make_async_copy(q_hbm.at[:, mine], qbuf.at[core], local_sem.at[3])
-    q_load.start()
-
     barrier = pltpu.get_barrier_semaphore()
 
     def greet_line(i, carry):
@@ -127,26 +114,43 @@
 
     lax.fori_loop(1, n_group, greet_group, 0)
 
-    meta[...] = jnp.zeros_like(meta)
-    meta[0:tok, 0:topk] = ids_ref[...].astype(F32)
-    meta[tok : 2 * tok, 0:topk] = gates_ref[...]
-    metag[a] = meta[...]
-    xg[a] = x_ref[...]
-    gg[a] = grad_ref[...]
-    head_k = pl.ds(pl.multiple_of(core * HD, HD), HD)
-    kbuf[g] = k_ref[:, head_k]
-    vbuf[g] = v_ref[:, head_k]
-
-    @pl.when(lax.rem(chip, 2) == 0)
+    half = qbuf.shape[2]
+    mine = pl.ds(pl.multiple_of(core * half, half), half)
+    theirs = pl.ds(pl.multiple_of(other * half, half), half)
+    head = pl.ds(pl.multiple_of(core * HD, HD), HD)
+    early = [
+        pltpu.make_async_copy(ids_hbm, idsg.at[a], local_sem.at[0]),
+        pltpu.make_async_copy(gates_hbm, gatesg.at[a], local_sem.at[1]),
+        pltpu.make_async_copy(x_hbm, xg.at[a], local_sem.at[2]),
+        pltpu.make_async_copy(grad_hbm, gg.at[a], local_sem.at[3]),
+    ]
+    own_heads = [
+        pltpu.make_async_copy(q_hbm.at[:, mine], qbuf.at[core], local_sem.at[4]),
+        pltpu.make_async_copy(k_hbm.at[:, head], kbuf.at[g], local_sem.at[5]),
+        pltpu.make_async_copy(v_hbm.at[:, head], vbuf.at[g], local_sem.at[6]),
+    ]
+    loads = [
+        pltpu.make_async_copy(wg_hbm, wg, local_sem.at[7]),
+        pltpu.make_async_copy(wu_hbm, wu, local_sem.at[8]),
+        pltpu.make_async_copy(wd_hbm, wd, local_sem.at[9]),
+    ]
+    for load in early + own_heads + loads:
+        load.start()
+
+    @pl.when((lax.rem(chip, 2) == 0) & (chunk > 2))
     def _():
-        for extra in (2, 3):
+        for extra in range(2, chunk):
             kbuf[2 * chip + extra] = jnp.zeros(kbuf.shape[1:], BF16)
             vbuf[2 * chip + extra] = jnp.zeros(vbuf.shape[1:], BF16)
 
     pl.semaphore_wait(barrier, 2 * (line - 1) + n_group - 1)
 
+    def distance(i):
+        odd = lax.rem(i, 2)
+        return odd * ((i + 1) // 2) + (1 - odd) * (line - i // 2)
+
     def along_a(f, source, dest, i):
-        p = lax.rem(a + i, line)
+        p = lax.rem(a + distance(i), line)
         return pltpu.make_async_remote_copy(
             src_ref=source(p),
             dst_ref=dest.at[a],
@@ -157,7 +161,7 @@
         )
 
     def along_b(f, source, dest, i):
-        p = lax.rem(b + i, line)
+        p = lax.rem(b + distance(i), line)
         return pltpu.make_async_remote_copy(
             src_ref=source(p),
             dst_ref=dest.at[b],
@@ -196,8 +200,38 @@
 
         lax.fori_loop(1, line, step, 0)
 
-    send_all(along_a, 0, lambda p: meta, metag)
-    send_all(along_a, 1, lambda p: x_ref, xg)
+    send_all(along_a, 0, lambda p: ids_hbm, idsg)
+    send_all(along_a, 9, lambda p: gates_hbm, gatesg)
+    send_all(along_a, 1, lambda p: x_hbm, xg)
+
+    n_up = line // 2
+    n_down = line - 1 - n_up
+    above = peer(lax.rem(a + 1, line), b)
+    below = peer(lax.rem(a + line - 1, line), b)
+
+    def ring_copy(f, up, step, source, dest):
+        n = step if up else n_up + step
+        return pltpu.make_async_remote_copy(
+            src_ref=source,
+            dst_ref=dest,
+            send_sem=line_send.at[f, n],
+            recv_sem=line_recv.at[f, n],
+            device_id=above if up else below,
+            device_id_type=MESH,
+        )
+
+    def gather_step(up, step):
+        p = lax.rem(a - step + line if up else a + step, line)
+        return ring_copy(2, up, step, grad_hbm if step == 0 else gg.at[p], gg.at[p])
+
+    def gather_send(step):
+        for up, n in ((True, n_up), (False, n_down)):
+            if step < n:
+                if step > 0:
+                    gather_step(up, step - 1).wait_recv()
+                gather_step(up, step).start()
+
+    gather_send(0)
 
     def kv_copy(j, what, source, dest):
         cols = pl.ds(pl.multiple_of(lax.rem(j, 2) * HD, HD), HD)
@@ -213,8 +247,8 @@
     def kv_start(j, carry):
         @pl.when(j != g)
         def _():
-            kv_copy(j, 0, k_ref, kbuf).start()
-            kv_copy(j, 1, v_ref, vbuf).start()
+            kv_copy(j, 0, k_hbm, kbuf).start()
+            kv_copy(j, 1, v_hbm, vbuf).start()
 
         return carry
 
@@ -228,13 +262,14 @@
         device_id_type=MESH,
     )
     q_send.start()
-    send_all(along_a, 2, lambda p: grad_ref, gg)
-
-    wait_all(0, a, metag)
+    for load in early:
+        load.wait()
+
+    wait_all(0, a, idsg)
+    wait_all(9, a, gatesg)
     n_tok = line * tok
-    lanes = meta.shape[1]
-    ids_t = metag[:, 0:tok, :].reshape(n_tok, lanes).T[0:topk]
-    gates_t = metag[:, tok : 2 * tok, :].reshape(n_tok, lanes).T[0:topk]
+    ids_t = jnp.concatenate([idsg[p] for p in range(line)], axis=1).astype(F32)
+    gates_t = jnp.concatenate([gatesg[p] for p in range(line)], axis=1)
     place = lax.broadcasted_iota(jnp.int32, (line, n_tok), 0)
     first = ((a // 2) * line + place) * 2 + lax.rem(a, 2)
     second = ((place // 2) * line + a) * 2 + lax.rem(place, 2)
@@ -284,10 +319,16 @@
             put_rows(dest, cols, picked)
         received[b] = dest[b]
 
+    for step in range(1, n_up - 1):
+        gather_send(step)
     wait_all(1, a, xg)
     pick(xg, sx, rx, None)
     send_all(along_b, 3, lambda p: sx.at[p], rx)
-    wait_all(2, a, gg)
+    if n_up > 1:
+        gather_send(n_up - 1)
+    gather_step(True, n_up - 1).wait_recv()
+    if n_down > 0:
+        gather_step(False, n_down - 1).wait_recv()
     pick(gg, sg, rg, gate_col)
     send_all(along_b, 4, lambda p: sg.at[p], rg)
 
@@ -311,6 +352,75 @@
         put_rows(so, cols, jnp.dot(act, wd[:, cols], preferred_element_type=F32))
     bo[b] = so[b]
     send_all(along_b, 5, lambda p: so.at[p], bo)
+
+    n_heads = half // HD
+    pos = k_hbm.shape[0]
+    q_rows = 2 * pos
+    keys = chunk * pos
+    exp_scale = 1.4426950408889634 / HD**0.5
+    n_chunks = (2 * chip + 1 + chunk) // chunk
+
+    def kv_wait(j):
+        @pl.when((j != g) & (j < 2 * chip + 2))
+        def _():
+            for what, dest in ((0, kbuf), (1, vbuf)):
+                pltpu.make_async_remote_copy(
+                    src_ref=dest.at[j],
+                    dst_ref=dest.at[j],
+                    send_sem=kv_send.at[what, j],
+                    recv_sem=kv_recv.at[what, j],
+                    device_id=sibling,
+                    device_id_type=MESH,
+                ).wait_recv()
+
+    def attend(j, diagonal):
+        def arrived(t, carry):
+            kv_wait(j * chunk + t)
+            return carry
+
+        lax.fori_loop(0, chunk, arrived, 0)
+        key_rows = kbuf[pl.ds(j * chunk, chunk)].reshape(keys, HD)
+        value_rows = vbuf[pl.ds(j * chunk, chunk)].reshape(keys, HD)
+        if diagonal:
+            ahead = lax.broadcasted_iota(jnp.int32, (q_rows, keys), 1) - lax.broadcasted_iota(
+                jnp.int32, (q_rows, keys), 0
+            )
+            seen = ahead <= q_rows * chip - keys * j
+        for h in range(n_heads):
+            cols = slice(h * HD, (h + 1) * HD)
+            query_rows = qbuf[:, :, cols].reshape(q_rows, HD)
+            scores = lax.dot_general(query_rows, key_rows, NT_DIMS, preferred_element_type=F32)
+            if diagonal:
+                scores = jnp.where(seen, scores, NEG)
+            top = jnp.max(scores, axis=1, keepdims=True)
+            m_new = jnp.broadcast_to(top, (q_rows, HD)) if diagonal else jnp.maximum(m_s[h], top)
+            total = None
+            weights = []
+            for c in range(0, keys, HD):
+                e = jnp.exp2((scores[:, c : c + HD] - m_new) * exp_scale)
+                total = e if total is None else total + e
+                weights.append(e.astype(BF16))
+            mixed = jnp.dot(jnp.concatenate(weights, axis=1), value_rows, preferred_element_type=F32)
+            if not diagonal:
+                alpha = jnp.exp2((m_s[h] - m_new) * exp_scale)
+                total = total + alpha * l_s[h]
+                mixed = mixed + alpha * acc_s[h]
+            m_s[h] = m_new
+            l_s[h] = total
+            acc_s[h] = mixed
+
+    def attend_down(first, last):
+        def step(i, carry):
+            attend(n_chunks - 1 - i, False)
+            return carry
+
+        lax.fori_loop(first, last, step, 0)
+
+    for load in own_heads:
+        load.wait()
+    q_send.wait_recv()
+    attend(n_chunks - 1, True)
+    attend_down(1, jnp.minimum(n_chunks, 2))
 
     wait_all(4, b, rg)
     grad_act = jnp.zeros((rows, ffe), F32)
@@ -332,63 +442,7 @@
     bi[b] = si[b]
     send_all(along_b, 6, lambda p: si.at[p], bi)
 
-    q_load.wait()
-    q_send.wait_recv()
-
-    def kv_wait(j, carry):
-        @pl.when(j != g)
-        def _():
-            for what, dest in ((0, kbuf), (1, vbuf)):
-                pltpu.make_async_remote_copy(
-                    src_ref=dest.at[j],
-                    dst_ref=dest.at[j],
-                    send_sem=kv_send.at[what, j],
-                    recv_sem=kv_recv.at[what, j],
-                    device_id=sibling,
-                    device_id_type=MESH,
-                ).wait_recv()
-
-        return carry
-
-    lax.fori_loop(0, 2 * chip + 2, kv_wait, 0)
-    n_heads = half // HD
-    pos = k_ref.shape[0]
-    q_rows = 2 * pos
-    keys = chunk * pos
-    m_s[...] = jnp.full_like(m_s, NEG)
-    l_s[...] = jnp.zeros_like(l_s)
-    acc_s[...] = jnp.zeros_like(acc_s)
-    exp_scale = 1.4426950408889634 / HD**0.5
-
-    def attend(j, carry):
-        key_rows = kbuf[pl.ds(j * chunk, chunk)].reshape(keys, HD)
-        value_rows = vbuf[pl.ds(j * chunk, chunk)].reshape(keys, HD)
-        ahead = lax.broadcasted_iota(jnp.int32, (q_rows, keys), 1) - lax.broadcasted_iota(
-            jnp.int32, (q_rows, keys), 0
-        )
-        seen = ahead <= q_rows * chip - keys * j
-        for h in range(n_heads):
-            cols = slice(h * HD, (h + 1) * HD)
-            query_rows = qbuf[:, :, cols].reshape(q_rows, HD)
-            scores = lax.dot_general(query_rows, key_rows, NT_DIMS, preferred_element_type=F32)
-            scores = jnp.where(seen, scores, NEG)
-            m_old = m_s[h]
-            m_new = jnp.maximum(m_old, jnp.max(scores, axis=1, keepdims=True))
-            alpha = jnp.exp2((m_old - m_new) * exp_scale)
-            total = alpha * l_s[h]
-            weights = []
-            for c in range(0, keys, HD):
-                e = jnp.exp2((scores[:, c : c + HD] - m_new) * exp_scale)
-                total = total + e
-                weights.append(e.astype(BF16))
-            m_s[h] = m_new
-            l_s[h] = total
-            acc_s[h] = alpha * acc_s[h] + jnp.dot(
-                jnp.concatenate(weights, axis=1), value_rows, preferred_element_type=F32
-            )
-        return carry
-
-    lax.fori_loop(0, (2 * chip + 1 + chunk) // chunk, attend, 0)
+    attend_down(2, n_chunks)
     for h in range(n_heads):
         cols = slice(h * HD, (h + 1) * HD)
         done = acc_s[h] / jnp.sum(l_s[h], axis=1, keepdims=True)
@@ -402,7 +456,7 @@
         device_id_type=MESH,
     )
     o_send.start()
-    o_store = pltpu.make_async_copy(obuf.at[core], attn_hbm.at[:, mine], local_sem.at[3])
+    o_store = pltpu.make_async_copy(obuf.at[core], attn_hbm.at[:, mine], local_sem.at[4])
     o_store.start()
 
     gated_hi = selg_s[...].astype(BF16)
@@ -411,7 +465,7 @@
     lo_t = gated_lo.astype(F32).T.astype(BF16)
     sel_t = sel.T.astype(BF16)
 
-    def mix(returned, dest, final, lefts):
+    def mix(returned, dest, lefts):
         for c in range(0, width, tile):
             cols = slice(c, c + tile)
             block = rows_of(returned, cols)
@@ -419,48 +473,85 @@
             for left in lefts[1:]:
                 mixed = mixed + jnp.dot(left, block, preferred_element_type=F32)
             dest[:, :, cols] = mixed.astype(BF16).reshape(line, tok, tile)
-        final[a] = dest[a]
 
     wait_all(5, b, bo)
-    mix(bo, po_s, po, (hi_t, lo_t))
-    send_all(along_a, 7, lambda p: po_s.at[p], po)
+    mix(bo, po_s, (hi_t, lo_t))
+
+    def sum_step(up, step):
+        p = lax.rem(a + n_up - step if up else a + line - n_down + step, line)
+        return p, ring_copy(7, up, step, po_s.at[p], po_r.at[step if up else n_up + step])
+
+    for step in range(n_up):
+        for up, n in ((True, n_up), (False, n_down)):
+            if step < n:
+                p, copy = sum_step(up, step)
+                if step > 0:
+                    sum_step(up, step - 1)[1].wait_recv()
+                    got = po_r[step - 1 if up else n_up + step - 1]
+                    po_s[p] = (po_s[p].astype(F32) + got.astype(F32)).astype(BF16)
+                copy.start()
+
     wait_all(6, b, bi)
-    mix(bi, pi_s, pi, (sel_t,))
+    mix(bi, pi_s, (sel_t,))
+    pi[a] = pi_s[a]
     send_all(along_a, 8, lambda p: pi_s.at[p], pi)
 
-    def add_up(final, out):
-        total = final[0].astype(F32)
-        for p in range(1, line):
-            total = total + final[p].astype(F32)
-        out[...] = total.astype(BF16)
-
-    wait_all(7, a, po)
-    add_up(po, mo_ref)
+    total = po_s[a].astype(F32)
+    sum_step(True, n_up - 1)[1].wait_recv()
+    total = total + po_r[n_up - 1].astype(F32)
+    if n_down > 0:
+        sum_step(False, n_down - 1)[1].wait_recv()
+        total = total + po_r[line - 2].astype(F32)
+    mo_ref[...] = total.astype(BF16)
+
     wait_all(8, a, pi)
-    add_up(pi, mg_ref)
+    total = pi[0].astype(F32)
+    for p in range(1, line):
+        total = total + pi[p].astype(F32)
+    mg_ref[...] = total.astype(BF16)
 
     o_store.wait()
     o_send.wait()
     q_send.wait_send()
-    sent_all(along_a, 0, lambda p: meta, metag)
-    sent_all(along_a, 1, lambda p: x_ref, xg)
-    sent_all(along_a, 2, lambda p: grad_ref, gg)
+    sent_all(along_a, 0, lambda p: ids_hbm, idsg)
+    sent_all(along_a, 9, lambda p: gates_hbm, gatesg)
+    sent_all(along_a, 1, lambda p: x_hbm, xg)
     sent_all(along_b, 3, lambda p: sx.at[p], rx)
     sent_all(along_b, 4, lambda p: sg.at[p], rg)
     sent_all(along_b, 5, lambda p: so.at[p], bo)
     sent_all(along_b, 6, lambda p: si.at[p], bi)
-    sent_all(along_a, 7, lambda p: po_s.at[p], po)
+    for up, n in ((True, n_up), (False, n_down)):
+        for step in range(n):
+            gather_step(up, step).wait_send()
+            sum_step(up, step)[1].wait_send()
     sent_all(along_a, 8, lambda p: pi_s.at[p], pi)
 
     def kv_sent(j, carry):
         @pl.when(j != g)
         def _():
-            kv_copy(j, 0, k_ref, kbuf).wait_send()
-            kv_copy(j, 1, v_ref, vbuf).wait_send()
+            kv_copy(j, 0, k_hbm, kbuf).wait_send()
+            kv_copy(j, 1, v_hbm, vbuf).wait_send()
 
         return carry
 
     lax.fori_loop(2 * chip, n_group, kv_sent, 0)
+
+
+def hand_over(pieces, attn, out, grad_in, attn_o, out_o, grad_o, attn_v, out_v, grad_v, came, went):
+    n = attn.shape[0] // pieces
+    parts = [
+        (attn.at[i * n : i * n + n], attn_v.at[i * n : i * n + n], attn_o.at[i * n : i * n + n])
+        for i in range(pieces)
+    ] + [(out, out_v, out_o), (grad_in, grad_v, grad_o)]
+    reads = [pltpu.make_async_copy(r, v, came.at[i]) for i, (r, v, _) in enumerate(parts)]
+    writes = [pltpu.make_async_copy(v, w, went.at[i]) for i, (_, v, w) in enumerate(parts)]
+    for read in reads:
+        read.start()
+    for read, write in zip(reads, writes):
+        read.wait()
+        write.start()
+    for write in writes:
+        write.wait()
 
 
 def shards(queries, keys, values, moe_x, expert_ids, gates, grad_out, w_gate, w_up, w_down):
@@ -487,7 +578,7 @@
             jax.ShapeDtypeStruct((tok, width), BF16),
             jax.ShapeDtypeStruct((tok, width), BF16),
         ),
-        in_specs=[vmem] * 6 + [hbm] * 4,
+        in_specs=[hbm] * 10,
         out_specs=(hbm, vmem, vmem),
         scratch_shapes=[
             pltpu.VMEM((width, ffe), BF16),
@@ -500,8 +591,8 @@
             state,
             state,
             state,
-            pltpu.VMEM((2 * tok, 128), F32),
-            pltpu.VMEM((line, 2 * tok, 128), F32),
+            pltpu.VMEM((line, topk, tok), jnp.int32),
+            pltpu.VMEM((line, topk, tok), F32),
             block,
             block,
             pltpu.VMEM((rows, n_tok), F32),
@@ -510,21 +601,21 @@
         + [slots] * 8
         + [block] * 4
         + [
-            pltpu.SemaphoreType.DMA((9, line)),
-            pltpu.SemaphoreType.DMA((9, line)),
+            pltpu.SemaphoreType.DMA((10, line)),
+            pltpu.SemaphoreType.DMA((10, line)),
             pltpu.SemaphoreType.DMA((2, n_group)),
             pltpu.SemaphoreType.DMA((2, n_group)),
             pltpu.SemaphoreType.DMA((2,)),
             pltpu.SemaphoreType.DMA((2,)),
-            pltpu.SemaphoreType.DMA((4,)),
+            pltpu.SemaphoreType.DMA((10,)),
         ],
         compiler_params=pltpu.CompilerParams(
             collective_id=0, has_side_effects=True, vmem_limit_bytes=60 * 1024 * 1024
         ),
     )(
         moe_x[0],
-        expert_ids[0],
-        gates[0],
+        expert_ids[0].T,
+        gates[0].T,
         grad_out[0],
         keys[0],
         values[0],
@@ -533,6 +624,20 @@
         w_up[0],
         w_down[0],
     )
+    pieces = 4
+    attn, out, grad_in = pl.pallas_call(
+        functools.partial(hand_over, pieces),
+        out_shape=tuple(jax.ShapeDtypeStruct(t.shape, BF16) for t in (attn, out, grad_in)),
+        in_specs=[hbm] * 3,
+        out_specs=(hbm,) * 3,
+        scratch_shapes=[
+            pltpu.VMEM(attn.shape, BF16),
+            pltpu.VMEM(out.shape, BF16),
+            pltpu.VMEM(out.shape, BF16),
+            pltpu.SemaphoreType.DMA((pieces + 2,)),
+            pltpu.SemaphoreType.DMA((pieces + 2,)),
+        ],
+    )(attn, out, grad_in)
     return attn[None], out[None], grad_in[None]
 
 

time: 101 us -> 97.1 us (0.961)
  the two profiles are of different devices: /device:TPU:10 before, /device:TPU:48 now
where the time goes in v2:
time: 97.1 us; the launch traced here: 96.9 us
  Pallas kernels  96.3 us (99%)
    pallas_call x1, Pallas kernels, shards(): pl.pallas_call(functools.partial(fused, (n_group, line, tok, topk, chunk)...  94.4 us

profile of v2, /device:TPU:48, one launch (start us, length us, event | category | flops | bytes accessed | tf_op | source)
XLA Modules:
  0.0 96.9 jit_solution(14767258591117572910)
XLA Ops:
  0.6 94.4 %shard_map.121 = (bf16[128,2048]{1,0:T(8,128)(2,1)}, bf16[16,2048]{1,0:T(8,128)(2,1)}, bf16[16,2048]{1,0:T(8,128)(2,1)}) custom-call(bf16[16,2048]{1,0:T(8,128)(2,1)} %bitcast.21, s32[8,16]{1,0:T(8,128)} %bitcast.25, f32[8,16]{1,0:T(8,128)} %bitcast.26, bf16[16,2048]{1,0:T(8,128)(2,1)} %bitcast.22, bf16[128,256]{1,0:T(8,128)(2,1)} %bitcast.23, ...), custom_call_target="tpu_custom_call" | custom-call | tf_op jit(solution)/shard_map/pallas_call | solution.py:574
  95.0 1.9 %shard_map.122 = (bf16[128,2048]{1,0:T(8,128)(2,1)}, bf16[16,2048]{1,0:T(8,128)(2,1)}, bf16[16,2048]{1,0:T(8,128)(2,1)}) custom-call(bf16[128,2048]{1,0:T(8,128)(2,1)} %get-tuple-element.9.attn, bf16[16,2048]{1,0:T(8,128)(2,1)} %get-tuple-element.10.out, bf16[16,2048]{1,0:T(8,128)(2,1)} %get-tuple-element.11.grad_in), custom_call_target="tpu_custom_call" | custom-call | tf_op jit(solution)/shard_map/pallas_call | solution.py:628

commit v3 on v2

--- a/solution.py
+++ b/solution.py
@@ -147,7 +147,7 @@
 
     def distance(i):
         odd = lax.rem(i, 2)
-        return odd * ((i + 1) // 2) + (1 - odd) * (line - i // 2)
+        return line // 2 + odd * (i // 2) - (1 - odd) * (i // 2)
 
     def along_a(f, source, dest, i):
         p = lax.rem(a + distance(i), line)
@@ -204,34 +204,35 @@
     send_all(along_a, 9, lambda p: gates_hbm, gatesg)
     send_all(along_a, 1, lambda p: x_hbm, xg)
 
-    n_up = line // 2
-    n_down = line - 1 - n_up
-    above = peer(lax.rem(a + 1, line), b)
-    below = peer(lax.rem(a + line - 1, line), b)
-
-    def ring_copy(f, up, step, source, dest):
-        n = step if up else n_up + step
+    near = {8: (1, -1, 2, -2), 4: (1, -1, 2), 2: (1,)}[line]
+    passed_on = {8: ((-2, 1), (-2, 2), (2, -1))}.get(line, ())
+
+    def at_a(offset):
+        return lax.rem(a + offset + line, line)
+
+    def grad_copy(n, source, p, offset):
         return pltpu.make_async_remote_copy(
             src_ref=source,
-            dst_ref=dest,
-            send_sem=line_send.at[f, n],
-            recv_sem=line_recv.at[f, n],
-            device_id=above if up else below,
+            dst_ref=gg.at[p],
+            send_sem=line_send.at[2, n],
+            recv_sem=line_recv.at[2, p],
+            device_id=peer(at_a(offset), b),
             device_id_type=MESH,
         )
 
-    def gather_step(up, step):
-        p = lax.rem(a - step + line if up else a + step, line)
-        return ring_copy(2, up, step, grad_hbm if step == 0 else gg.at[p], gg.at[p])
-
-    def gather_send(step):
-        for up, n in ((True, n_up), (False, n_down)):
-            if step < n:
-                if step > 0:
-                    gather_step(up, step - 1).wait_recv()
-                gather_step(up, step).start()
-
-    gather_send(0)
+    def grad_near(n):
+        return grad_copy(n, grad_hbm, a, near[n])
+
+    def grad_pass(n):
+        p = at_a(passed_on[n][0])
+        return grad_copy(len(near) + n, gg.at[p], p, passed_on[n][1])
+
+    def grad_wait(offset):
+        p = at_a(offset)
+        grad_copy(0, gg.at[p], p, 1).wait_recv()
+
+    for n in range(len(near)):
+        grad_near(n).start()
 
     def kv_copy(j, what, source, dest):
         cols = pl.ds(pl.multiple_of(lax.rem(j, 2) * HD, HD), HD)
@@ -296,7 +297,7 @@
     sel_b = sel.astype(BF16)
     gate_col = jnp.sum(selg_s[...], axis=1, keepdims=True)
 
-    tile = min(width, 512)
+    tile = min(width // 2, 512)
 
     def rows_of(ref, cols):
         return jnp.concatenate(
@@ -319,16 +320,17 @@
             put_rows(dest, cols, picked)
         received[b] = dest[b]
 
-    for step in range(1, n_up - 1):
-        gather_send(step)
     wait_all(1, a, xg)
     pick(xg, sx, rx, None)
     send_all(along_b, 3, lambda p: sx.at[p], rx)
-    if n_up > 1:
-        gather_send(n_up - 1)
-    gather_step(True, n_up - 1).wait_recv()
-    if n_down > 0:
-        gather_step(False, n_down - 1).wait_recv()
+    first_seen = sorted({offset for offset, _ in passed_on})
+    for offset in first_seen:
+        grad_wait(offset)
+    for n in range(len(passed_on)):
+        grad_pass(n).start()
+    for offset in range(1, line):
+        if offset not in [o % line for o in first_seen]:
+            grad_wait(offset)
     pick(gg, sg, rg, gate_col)
     send_all(along_b, 4, lambda p: sg.at[p], rg)
 
@@ -431,16 +433,18 @@
         )
     grad_gate = (grad_act * hup * sig * (1.0 + hgate * (1.0 - sig))).astype(BF16)
     grad_up = (grad_act * silu).astype(BF16)
-    for c in range(0, width, tile):
-        cols = slice(c, c + tile)
-        put_rows(
-            si,
-            cols,
-            lax.dot_general(grad_gate, wg[cols, :], NT_DIMS, preferred_element_type=F32)
-            + lax.dot_general(grad_up, wu[cols, :], NT_DIMS, preferred_element_type=F32),
-        )
-    bi[b] = si[b]
-    send_all(along_b, 6, lambda p: si.at[p], bi)
+    wide = width // 2
+    for h in range(2):
+        for c in range(0, wide, tile):
+            cols = slice(h * wide + c, h * wide + c + tile)
+            put_rows(
+                si.at[h],
+                slice(c, c + tile),
+                lax.dot_general(grad_gate, wg[cols, :], NT_DIMS, preferred_element_type=F32)
+                + lax.dot_general(grad_up, wu[cols, :], NT_DIMS, preferred_element_type=F32),
+            )
+        bi[h, b] = si[h, b]
+        send_all(along_b, (6, 10)[h], lambda p, h=h: si.at[h, p], bi.at[h])
 
     attend_down(2, n_chunks)
     for h in range(n_heads):
@@ -466,7 +470,7 @@
     sel_t = sel.T.astype(BF16)
 
     def mix(returned, dest, lefts):
-        for c in range(0, width, tile):
+        for c in range(0, returned.shape[-1], tile):
             cols = slice(c, c + tile)
             block = rows_of(returned, cols)
             mixed = jnp.dot(lefts[0], block, preferred_element_type=F32)
@@ -474,41 +478,55 @@
                 mixed = mixed + jnp.dot(left, block, preferred_element_type=F32)
             dest[:, :, cols] = mixed.astype(BF16).reshape(line, tok, tile)
 
+    sums = {
+        8: ((0, 1, 1), (1, -1, -1), (2, -3, -1), (3, 4, -2), (4, 3, 1)),
+        4: ((0, 1, 1), (1, -1, -1), (2, 2, 2)),
+        2: ((0, 1, 1),),
+    }[line]
+    added = {8: ((5, -2, (2, 3)), (6, 2, (4,)))}.get(line, ())
+    half_way = [t for _, _, slots in added for t in slots]
+
+    def sum_copy(slot, home, offset):
+        return pltpu.make_async_remote_copy(
+            src_ref=po_s.at[at_a(home)],
+            dst_ref=po_r.at[slot],
+            send_sem=line_send.at[7, slot],
+            recv_sem=line_recv.at[7, slot],
+            device_id=peer(at_a(offset), b),
+            device_id_type=MESH,
+        )
+
     wait_all(5, b, bo)
     mix(bo, po_s, (hi_t, lo_t))
-
-    def sum_step(up, step):
-        p = lax.rem(a + n_up - step if up else a + line - n_down + step, line)
-        return p, ring_copy(7, up, step, po_s.at[p], po_r.at[step if up else n_up + step])
-
-    for step in range(n_up):
-        for up, n in ((True, n_up), (False, n_down)):
-            if step < n:
-                p, copy = sum_step(up, step)
-                if step > 0:
-                    sum_step(up, step - 1)[1].wait_recv()
-                    got = po_r[step - 1 if up else n_up + step - 1]
-                    po_s[p] = (po_s[p].astype(F32) + got.astype(F32)).astype(BF16)
-                copy.start()
-
-    wait_all(6, b, bi)
-    mix(bi, pi_s, (sel_t,))
-    pi[a] = pi_s[a]
-    send_all(along_a, 8, lambda p: pi_s.at[p], pi)
-
+    for slot, home, offset in sums:
+        sum_copy(slot, home, offset).start()
+
+    for h in range(2):
+        wait_all((6, 10)[h], b, bi.at[h])
+        mix(bi.at[h], pi_s.at[h], (sel_t,))
+        pi[h, a] = pi_s[h, a]
+        send_all(along_a, (8, 11)[h], lambda p, h=h: pi_s.at[h, p], pi.at[h])
+
+    for slot, home, slots in added:
+        total = po_s[at_a(home)].astype(F32)
+        for t in slots:
+            sum_copy(t, 0, 1).wait_recv()
+            total = total + po_r[t].astype(F32)
+        po_s[at_a(home)] = total.astype(BF16)
+        sum_copy(slot, home, home).start()
     total = po_s[a].astype(F32)
-    sum_step(True, n_up - 1)[1].wait_recv()
-    total = total + po_r[n_up - 1].astype(F32)
-    if n_down > 0:
-        sum_step(False, n_down - 1)[1].wait_recv()
-        total = total + po_r[line - 2].astype(F32)
+    for slot in [m[0] for m in sums] + [m[0] for m in added]:
+        if slot not in half_way:
+            sum_copy(slot, 0, 1).wait_recv()
+            total = total + po_r[slot].astype(F32)
     mo_ref[...] = total.astype(BF16)
 
-    wait_all(8, a, pi)
-    total = pi[0].astype(F32)
-    for p in range(1, line):
-        total = total + pi[p].astype(F32)
-    mg_ref[...] = total.astype(BF16)
+    for h in range(2):
+        wait_all((8, 11)[h], a, pi.at[h])
+        total = pi[h, 0].astype(F32)
+        for p in range(1, line):
+            total = total + pi[h, p].astype(F32)
+        mg_ref[:, h * wide : (h + 1) * wide] = total.astype(BF16)
 
     o_store.wait()
     o_send.wait()
@@ -519,12 +537,17 @@
     sent_all(along_b, 3, lambda p: sx.at[p], rx)
     sent_all(along_b, 4, lambda p: sg.at[p], rg)
     sent_all(along_b, 5, lambda p: so.at[p], bo)
-    sent_all(along_b, 6, lambda p: si.at[p], bi)
-    for up, n in ((True, n_up), (False, n_down)):
-        for step in range(n):
-            gather_step(up, step).wait_send()
-            sum_step(up, step)[1].wait_send()
-    sent_all(along_a, 8, lambda p: pi_s.at[p], pi)
+    for h in range(2):
+        sent_all(along_b, (6, 10)[h], lambda p, h=h: si.at[h, p], bi.at[h])
+        sent_all(along_a, (8, 11)[h], lambda p, h=h: pi_s.at[h, p], pi.at[h])
+    for n in range(len(near)):
+        grad_near(n).wait_send()
+    for n in range(len(passed_on)):
+        grad_pass(n).wait_send()
+    for slot, home, offset in sums:
+        sum_copy(slot, home, offset).wait_send()
+    for slot, home, _ in added:
+        sum_copy(slot, home, home).wait_send()
 
     def kv_sent(j, carry):
         @pl.when(j != g)
@@ -569,7 +592,9 @@
     vmem = pl.BlockSpec(memory_space=pltpu.VMEM)
     hbm = pl.BlockSpec(memory_space=pl.ANY)
     slots = pltpu.VMEM((line, CAP, line, width), BF16)
+    slot_halves = pltpu.VMEM((2, line, CAP, line, width // 2), BF16)
     block = pltpu.VMEM((line, tok, width), BF16)
+    halves = pltpu.VMEM((2, line, tok, width // 2), BF16)
     state = pltpu.VMEM((n_heads, 2 * pos, HD), F32)
     attn, out, grad_in = pl.pallas_call(
         functools.partial(fused, (n_group, line, tok, topk, chunk)),
@@ -598,11 +623,12 @@
             pltpu.VMEM((rows, n_tok), F32),
             pltpu.VMEM((rows, n_tok), F32),
         ]
-        + [slots] * 8
-        + [block] * 4
+        + [slots] * 5
+        + [slot_halves, slots, slot_halves]
+        + [block, halves, block, halves]
         + [
-            pltpu.SemaphoreType.DMA((10, line)),
-            pltpu.SemaphoreType.DMA((10, line)),
+            pltpu.SemaphoreType.DMA((12, line)),
+            pltpu.SemaphoreType.DMA((12, line)),
             pltpu.SemaphoreType.DMA((2, n_group)),
             pltpu.SemaphoreType.DMA((2, n_group)),
             pltpu.SemaphoreType.DMA((2,)),

time: 97.1 us -> 94.9 us (0.977)
  the two profiles are of different devices: /device:TPU:48 before, /device:TPU:14 now
where the time goes in v3:
time: 94.9 us; the launch traced here: 94.7 us
  Pallas kernels  94.1 us (99%)
    pallas_call x1, Pallas kernels, shards(): pl.pallas_call(functools.partial(fused, (n_group, line, tok, topk, chunk)...  92.2 us

profile of v3, /device:TPU:14, one launch (start us, length us, event | category | flops | bytes accessed | tf_op | source)
XLA Modules:
  0.0 94.7 jit_solution(18151792821011030044)
XLA Ops:
  0.6 92.2 %shard_map.121 = (bf16[128,2048]{1,0:T(8,128)(2,1)}, bf16[16,2048]{1,0:T(8,128)(2,1)}, bf16[16,2048]{1,0:T(8,128)(2,1)}) custom-call(bf16[16,2048]{1,0:T(8,128)(2,1)} %bitcast.21, s32[8,16]{1,0:T(8,128)} %bitcast.25, f32[8,16]{1,0:T(8,128)} %bitcast.26, bf16[16,2048]{1,0:T(8,128)(2,1)} %bitcast.22, bf16[128,256]{1,0:T(8,128)(2,1)} %bitcast.23, ...), custom_call_target="tpu_custom_call" | custom-call | tf_op jit(solution)/shard_map/pallas_call | solution.py:599
  92.8 1.9 %shard_map.122 = (bf16[128,2048]{1,0:T(8,128)(2,1)}, bf16[16,2048]{1,0:T(8,128)(2,1)}, bf16[16,2048]{1,0:T(8,128)(2,1)}) custom-call(bf16[128,2048]{1,0:T(8,128)(2,1)} %get-tuple-element.9.attn, bf16[16,2048]{1,0:T(8,128)(2,1)} %get-tuple-element.10.out, bf16[16,2048]{1,0:T(8,128)(2,1)} %get-tuple-element.11.grad_in), custom_call_target="tpu_custom_call" | custom-call | tf_op jit(solution)/shard_map/pallas_call | solution.py:654

commit v4 on v3

v4 whole, which is shorter than its diff:
```python
import functools

import jax
import jax.numpy as jnp
from jax import lax
from jax.experimental import pallas as pl
from jax.experimental.pallas import tpu as pltpu
from jax.sharding import PartitionSpec as P

H = 32
KVH = 4
HD = 128
CAP = 3
LINE = 8
CHUNK = 4
MESH = pl.DeviceIdType.MESH
NT_DIMS = (((1,), (1,)), ((), ()))
F32 = jnp.float32
BF16 = jnp.bfloat16
NEG = -1e30
FAMILIES = 10


def fused(
    cfg,
    x_hbm,
    ids_hbm,
    gates_hbm,
    grad_hbm,
    k_hbm,
    v_hbm,
    q_hbm,
    wg_hbm,
    wu_hbm,
    wd_hbm,
    attn_hbm,
    mo_ref,
    mg_ref,
    wg,
    wu,
    wd,
    qbuf,
    kbuf,
    vbuf,
    obuf,
    m_s,
    l_s,
    acc_s,
    idsg,
    gatesg,
    xg,
    gg,
    sel_s,
    selg_s,
    sx,
    sg,
    rx,
    rg,
    so,
    si,
    bo,
    bi,
    po_s,
    pi_s,
    po_r,
    pi,
    line_send,
    line_recv,
    kv_send,
    kv_recv,
    pair_send,
    pair_recv,
    local_sem,
):
    n_group, line, tok, topk, chunk = cfg
    chips = n_group // 2
    rows = line * CAP * line
    part = CAP * line
    width = x_hbm.shape[1]
    wide = width // 2
    halves = (0, 1)
    cols_of = [slice(h * wide, (h + 1) * wide) for h in halves]
    g = lax.axis_index("group")
    seq = lax.axis_index("seq")
    tp = lax.axis_index("tp")
    core = lax.rem(g, 2)
    chip = g // 2
    y = lax.rem(seq, line)
    z = (seq // line) * 2 + tp
    me_a = (z, y)
    me_b = (y, z)

    def at(yy, zz):
        return (g, (zz // 2) * line + yy, lax.rem(zz, 2))

    def a_peer(h, p):
        return at(p, z) if h else at(y, p)

    def b_peer(h, p):
        return at(y, p) if h else at(p, z)

    def in_group(j):
        return (j, seq, tp)

    other = 1 - core
    sibling = in_group(2 * chip + other)

    barrier = pltpu.get_barrier_semaphore()

    def greet_line(i, carry):
        for h in halves:
            p = lax.rem(me_a[h] + i, line)
            pl.semaphore_signal(barrier, 1, device_id=a_peer(h, p), device_id_type=MESH)
        return carry

    lax.fori_loop(1, line, greet_line, 0)

    def greet_group(i, carry):
        pl.semaphore_signal(
            barrier, 1, device_id=in_group(lax.rem(g + i, n_group)), device_id_type=MESH
        )
        return carry

    lax.fori_loop(1, n_group, greet_group, 0)

    half = qbuf.shape[2]
    mine = pl.ds(pl.multiple_of(core * half, half), half)
    theirs = pl.ds(pl.multiple_of(other * half, half), half)
    head = pl.ds(pl.multiple_of(core * HD, HD), HD)
    early = []
    for h in halves:
        early += [
            pltpu.make_async_copy(ids_hbm, idsg.at[h, me_a[h]], local_sem.at[6 + 4 * h]),
            pltpu.make_async_copy(gates_hbm, gatesg.at[h, me_a[h]], local_sem.at[7 + 4 * h]),
            pltpu.make_async_copy(x_hbm.at[:, cols_of[h]], xg.at[h, me_a[h]], local_sem.at[8 + 4 * h]),
            pltpu.make_async_copy(grad_hbm.at[:, cols_of[h]], gg.at[h, me_a[h]], local_sem.at[9 + 4 * h]),
        ]
    own_heads = [
        pltpu.make_async_copy(q_hbm.at[:, mine], qbuf.at[core], local_sem.at[0]),
        pltpu.make_async_copy(k_hbm.at[:, head], kbuf.at[g], local_sem.at[1]),
        pltpu.make_async_copy(v_hbm.at[:, head], vbuf.at[g], local_sem.at[2]),
    ]
    loads = [
        pltpu.make_async_copy(wg_hbm, wg, local_sem.at[3]),
        pltpu.make_async_copy(wu_hbm, wu, local_sem.at[4]),
        pltpu.make_async_copy(wd_hbm, wd, local_sem.at[5]),
    ]
    for load in early + own_heads + loads:
        load.start()

    @pl.when((lax.rem(chip, 2) == 0) & (chunk > 2))
    def _():
        for extra in range(2, chunk):
            kbuf[2 * chip + extra] = jnp.zeros(kbuf.shape[1:], BF16)
            vbuf[2 * chip + extra] = jnp.zeros(vbuf.shape[1:], BF16)

    pl.semaphore_wait(barrier, 2 * (line - 1) + n_group - 1)

    def distance(i):
        odd = lax.rem(i, 2)
        return line // 2 + odd * (i // 2) - (1 - odd) * (i // 2)

    def line_copy(on_a, f, source, dest, h, i):
        me = me_a[h] if on_a else me_b[h]
        p = lax.rem(me + distance(i), line)
        return pltpu.make_async_remote_copy(
            src_ref=source(h, p),
            dst_ref=dest.at[h, me],
            send_sem=line_send.at[FAMILIES * h + f, i],
            recv_sem=line_recv.at[FAMILIES * h + f, me],
            device_id=(a_peer if on_a else b_peer)(h, p),
            device_id_type=MESH,
        )

    def send_all(on_a, f, source, dest, which=halves):
        def step(i, carry):
            for h in which:
                line_copy(on_a, f, source, dest, h, i).start()
            return carry

        lax.fori_loop(1, line, step, 0)

    def sent_all(on_a, f, source, dest):
        def step(i, carry):
            for h in halves:
                line_copy(on_a, f, source, dest, h, i).wait_send()
            return carry

        lax.fori_loop(1, line, step, 0)

    def wait_all(on_a, f, dest, h):
        me = me_a[h] if on_a else me_b[h]

        def step(i, carry):
            p = lax.rem(me + i, line)
            pltpu.make_async_remote_copy(
                src_ref=dest.at[h, p],
                dst_ref=dest.at[h, p],
                send_sem=line_send.at[FAMILIES * h + f, i],
                recv_sem=line_recv.at[FAMILIES * h + f, p],
                device_id=sibling,
                device_id_type=MESH,
            ).wait_recv()
            return carry

        lax.fori_loop(1, line, step, 0)

    def ids_from(h, p):
        return ids_hbm

    def gates_from(h, p):
        return gates_hbm

    def x_from(h, p):
        return x_hbm.at[:, cols_of[h]]

    def block_of(ref):
        return lambda h, p: ref.at[h, p]

    send_all(True, 0, ids_from, idsg)
    send_all(True, 9, gates_from, gatesg)
    send_all(True, 1, x_from, xg)

    near = {8: (4, 3, -3, 2, -2, 1, -1), 4: (1, -1, 2), 2: (1,)}[line]
    passed_on = ()

    def at_a(h, offset):
        return lax.rem(me_a[h] + offset + line, line)

    def grad_copy(h, n, source, p, offset):
        return pltpu.make_async_remote_copy(
            src_ref=source,
            dst_ref=gg.at[h, p],
            send_sem=line_send.at[FAMILIES * h + 2, n],
            recv_sem=line_recv.at[FAMILIES * h + 2, p],
            device_id=a_peer(h, at_a(h, offset)),
            device_id_type=MESH,
        )

    def grad_near(h, n):
        return grad_copy(h, n, grad_hbm.at[:, cols_of[h]], me_a[h], near[n])

    def grad_pass(h, n):
        p = at_a(h, passed_on[n][0])
        return grad_copy(h, len(near) + n, gg.at[h, p], p, passed_on[n][1])

    def grad_wait(h, offset):
        p = at_a(h, offset)
        grad_copy(h, 0, gg.at[h, p], p, 1).wait_recv()

    for n in range(len(near)):
        for h in halves:
            grad_near(h, n).start()

    def kv_copy(j, what, source, dest):
        cols = pl.ds(pl.multiple_of(lax.rem(j, 2) * HD, HD), HD)
        return pltpu.make_async_remote_copy(
            src_ref=source.at[:, cols],
            dst_ref=dest.at[g],
            send_sem=kv_send.at[what, j],
            recv_sem=kv_recv.at[what, g],
            device_id=in_group(j),
            device_id_type=MESH,
        )

    def kv_start(j, carry):
        @pl.when(j != g)
        def _():
            kv_copy(j, 0, k_hbm, kbuf).start()
            kv_copy(j, 1, v_hbm, vbuf).start()

        return carry

    lax.fori_loop(2 * chip, n_group, kv_start, 0)
    q_send = pltpu.make_async_remote_copy(
        src_ref=q_hbm.at[:, theirs],
        dst_ref=qbuf.at[core],
        send_sem=pair_send.at[0],
        recv_sem=pair_recv.at[0],
        device_id=sibling,
        device_id_type=MESH,
    )
    q_send.start()
    for load in early:
        load.wait()

    n_tok = line * tok
    place = lax.broadcasted_iota(jnp.int32, (line, n_tok), 0)
    t_row = lax.broadcasted_iota(jnp.int32, (n_tok, n_tok), 0)
    t_col = lax.broadcasted_iota(jnp.int32, (n_tok, n_tok), 1)
    earlier = jnp.where((t_row // tok == t_col // tok) & (t_row < t_col), 1.0, 0.0).astype(BF16)
    own_block = jnp.where(place == lax.broadcasted_iota(jnp.int32, (line, n_tok), 1) // tok, 1.0, 0.0)
    experts = (
        ((z // 2) * line + place) * 2 + lax.rem(z, 2),
        ((place // 2) * line + y) * 2 + lax.rem(place, 2),
    )
    for h in halves:
        wait_all(True, 0, idsg, h)
        wait_all(True, 9, gatesg, h)
        ids_t = jnp.concatenate([idsg[h, p] for p in range(line)], axis=1)
        gates_t = jnp.concatenate([gatesg[h, p] for p in range(line)], axis=1)
        named = jnp.zeros((line, n_tok), F32)
        gate = jnp.zeros((line, n_tok), F32)
        for k in range(topk):
            hit = jnp.where(ids_t[k : k + 1] == experts[h], 1.0, 0.0)
            named = named + hit
            gate = gate + hit * gates_t[k : k + 1]
        rank = jnp.dot(named.astype(BF16), earlier, preferred_element_type=F32)
        for s in range(CAP):
            slot = jnp.where(rank == s, named, 0.0)
            slot_gate = slot * gate
            for d in range(line):
                r = pl.ds(d * part + s * line, line)
                sel_s[h, r] = own_block * slot[d : d + 1]
                selg_s[h, r] = own_block * slot_gate[d : d + 1]

    shift = lax.broadcasted_iota(jnp.int32, (line, rows), 1) - part * lax.broadcasted_iota(
        jnp.int32, (line, rows), 0
    )
    swap = jnp.concatenate(
        [jnp.where(shift == s * line + d, 1.0, 0.0) for d in range(line) for s in range(CAP)], axis=0
    ).astype(BF16)

    def swapped(value):
        return jnp.dot(swap, value, preferred_element_type=F32).astype(BF16)

    tile = min(wide, 512)

    def rows_of(ref, h, cols):
        return jnp.concatenate(
            [ref[h, d, s, :, cols].astype(F32) for d in range(line) for s in range(CAP)], axis=0
        ).astype(BF16)

    def put_rows(ref, h, cols, value):
        for d in range(line):
            for s in range(CAP):
                r = d * part + s * line
                ref[h, d, s, :, cols] = value[r : r + line].astype(BF16)

    def pick(h, source, dest, received, scaled):
        left = sel_s[h].astype(BF16)
        if scaled:
            scale = jnp.sum(selg_s[h], axis=1, keepdims=True)
        for c in range(0, wide, tile):
            cols = slice(c, c + tile)
            block = source[h, :, :, cols].reshape(n_tok, tile)
            picked = jnp.dot(left, block, preferred_element_type=F32)
            if scaled:
                picked = picked * scale
            put_rows(dest, h, cols, picked)
        received[h, me_b[h]] = dest[h, me_b[h]]

    wait_all(True, 1, xg, 0)
    first_seen = sorted({offset for offset, _ in passed_on})
    for h in halves:
        for offset in first_seen:
            grad_wait(h, offset)
        for n in range(len(passed_on)):
            grad_pass(h, n).start()

    for h in halves:
        if h:
            wait_all(True, 1, xg, h)
        pick(h, xg, sx, rx, False)
        send_all(False, 3, block_of(sx), rx, (h,))

    for h in halves:
        for offset in range(1, line):
            if offset not in [o % line for o in first_seen]:
                grad_wait(h, offset)
        pick(h, gg, sg, rg, True)
        send_all(False, 4, block_of(sg), rg, (h,))

    for load in loads:
        load.wait()

    ffe = wg.shape[1]
    hgate = jnp.zeros((rows, ffe), F32)
    hup = jnp.zeros((rows, ffe), F32)
    for h in halves:
        wait_all(False, 3, rx, h)
        for c in range(0, wide, tile):
            token_rows = rows_of(rx, h, slice(c, c + tile))
            if h:
                token_rows = swapped(token_rows)
            depth = slice(h * wide + c, h * wide + c + tile)
            hgate = hgate + jnp.dot(token_rows, wg[depth, :], preferred_element_type=F32)
            hup = hup + jnp.dot(token_rows, wu[depth, :], preferred_element_type=F32)
    sig = 1.0 / (1.0 + jnp.exp(-hgate))
    silu = hgate * sig
    act = (silu * hup).astype(BF16)
    for h in halves:
        left = swapped(act) if h else act
        for c in range(0, wide, tile):
            depth = slice(h * wide + c, h * wide + c + tile)
            put_rows(
                so, h, slice(c, c + tile), jnp.dot(left, wd[:, depth], preferred_element_type=F32)
            )
        bo[h, me_b[h]] = so[h, me_b[h]]
        send_all(False, 5, block_of(so), bo, (h,))

    n_heads = half // HD
    pos = k_hbm.shape[0]
    q_rows = 2 * pos
    keys = chunk * pos
    exp_scale = 1.4426950408889634 / HD**0.5
    n_chunks = (2 * chip + 1 + chunk) // chunk

    def kv_wait(j):
        @pl.when((j != g) & (j < 2 * chip + 2))
        def _():
            for what, dest in ((0, kbuf), (1, vbuf)):
                pltpu.make_async_remote_copy(
                    src_ref=dest.at[j],
                    dst_ref=dest.at[j],
                    send_sem=kv_send.at[what, j],
                    recv_sem=kv_recv.at[what, j],
                    device_id=sibling,
                    device_id_type=MESH,
                ).wait_recv()

    def attend(j, diagonal):
        def arrived(t, carry):
            kv_wait(j * chunk + t)
            return carry

        lax.fori_loop(0, chunk, arrived, 0)
        key_rows = kbuf[pl.ds(j * chunk, chunk)].reshape(keys, HD)
        value_rows = vbuf[pl.ds(j * chunk, chunk)].reshape(keys, HD)
        if diagonal:
            ahead = lax.broadcasted_iota(jnp.int32, (q_rows, keys), 1) - lax.broadcasted_iota(
                jnp.int32, (q_rows, keys), 0
            )
            seen = ahead <= q_rows * chip - keys * j
        for h in range(n_heads):
            cols = slice(h * HD, (h + 1) * HD)
            query_rows = qbuf[:, :, cols].reshape(q_rows, HD)
            scores = lax.dot_general(query_rows, key_rows, NT_DIMS, preferred_element_type=F32)
            if diagonal:
                scores = jnp.where(seen, scores, NEG)
            top = jnp.max(scores, axis=1, keepdims=True)
            m_new = jnp.broadcast_to(top, (q_rows, HD)) if diagonal else jnp.maximum(m_s[h], top)
            total = None
            weights = []
            for c in range(0, keys, HD):
                e = jnp.exp2((scores[:, c : c + HD] - m_new) * exp_scale)
                total = e if total is None else total + e
                weights.append(e.astype(BF16))
            mixed = jnp.dot(jnp.concatenate(weights, axis=1), value_rows, preferred_element_type=F32)
            if not diagonal:
                alpha = jnp.exp2((m_s[h] - m_new) * exp_scale)
                total = total + alpha * l_s[h]
                mixed = mixed + alpha * acc_s[h]
            m_s[h] = m_new
            l_s[h] = total
            acc_s[h] = mixed

    def attend_down(first, last):
        def step(i, carry):
            attend(n_chunks - 1 - i, False)
            return carry

        lax.fori_loop(first, last, step, 0)

    for load in own_heads:
        load.wait()
    q_send.wait_recv()
    attend(n_chunks - 1, True)
    attend_down(1, jnp.minimum(n_chunks, 2))

    grad_act = jnp.zeros((rows, ffe), F32)
    for h in halves:
        wait_all(False, 4, rg, h)
        for c in range(0, wide, tile):
            grad_rows = rows_of(rg, h, slice(c, c + tile))
            if h:
                grad_rows = swapped(grad_rows)
            depth = slice(h * wide + c, h * wide + c + tile)
            grad_act = grad_act + lax.dot_general(
                grad_rows, wd[:, depth], NT_DIMS, preferred_element_type=F32
            )
    grad_gate = (grad_act * hup * sig * (1.0 + hgate * (1.0 - sig))).astype(BF16)
    grad_up = (grad_act * silu).astype(BF16)
    for h in halves:
        if h:
            grad_gate, grad_up = swapped(grad_gate), swapped(grad_up)
        for c in range(0, wide, tile):
            depth = slice(h * wide + c, h * wide + c + tile)
            put_rows(
                si,
                h,
                slice(c, c + tile),
                lax.dot_general(grad_gate, wg[depth, :], NT_DIMS, preferred_element_type=F32)
                + lax.dot_general(grad_up, wu[depth, :], NT_DIMS, preferred_element_type=F32),
            )
        bi[h, me_b[h]] = si[h, me_b[h]]
        send_all(False, 6, block_of(si), bi, (h,))

    attend_down(2, n_chunks)
    for h in range(n_heads):
        cols = slice(h * HD, (h + 1) * HD)
        done = acc_s[h] / jnp.sum(l_s[h], axis=1, keepdims=True)
        obuf[:, :, cols] = done.astype(BF16).reshape(2, pos, HD)
    o_send = pltpu.make_async_remote_copy(
        src_ref=obuf.at[other],
        dst_ref=attn_hbm.at[:, mine],
        send_sem=pair_send.at[1],
        recv_sem=pair_recv.at[1],
        device_id=sibling,
        device_id_type=MESH,
    )
    o_send.start()
    o_store = pltpu.make_async_copy(obuf.at[core], attn_hbm.at[:, mine], local_sem.at[0])
    o_store.start()

    def mix(h, returned, dest, lefts):
        for c in range(0, wide, tile):
            cols = slice(c, c + tile)
            block = rows_of(returned, h, cols)
            mixed = jnp.dot(lefts[0], block, preferred_element_type=F32)
            for left in lefts[1:]:
                mixed = mixed + jnp.dot(left, block, preferred_element_type=F32)
            dest[h, :, :, cols] = mixed.astype(BF16).reshape(line, tok, tile)

    sums = {
        8: ((0, 1, 1), (1, -1, -1), (2, -3, -1), (3, 4, -2), (4, 3, 1)),
        4: ((0, 1, 1), (1, -1, -1), (2, 2, 2)),
        2: ((0, 1, 1),),
    }[line]
    added = {8: ((5, -2, (2, 3)), (6, 2, (4,)))}.get(line, ())
    half_way = [t for _, _, slots in added for t in slots]

    def sum_copy(h, slot, home, offset):
        return pltpu.make_async_remote_copy(
            src_ref=po_s.at[h, at_a(h, home)],
            dst_ref=po_r.at[h, slot],
            send_sem=line_send.at[FAMILIES * h + 7, slot],
            recv_sem=line_recv.at[FAMILIES * h + 7, slot],
            device_id=a_peer(h, at_a(h, offset)),
            device_id_type=MESH,
        )

    for h in halves:
        hi = selg_s[h].astype(BF16).astype(F32)
        lo = selg_s[h] - hi
        wait_all(False, 5, bo, h)
        mix(h, bo, po_s, (hi.T.astype(BF16), lo.T.astype(BF16)))
        for slot, home, offset in sums:
            sum_copy(h, slot, home, offset).start()

    for h in halves:
        wait_all(False, 6, bi, h)
        mix(h, bi, pi_s, (sel_s[h].T.astype(BF16),))
        pi[h, me_a[h]] = pi_s[h, me_a[h]]
        send_all(True, 8, block_of(pi_s), pi, (h,))

    for h in halves:
        for slot, home, slots in added:
            total = po_s[h, at_a(h, home)].astype(F32)
            for t in slots:
                sum_copy(h, t, 0, 1).wait_recv()
                total = total + po_r[h, t].astype(F32)
            po_s[h, at_a(h, home)] = total.astype(BF16)
            sum_copy(h, slot, home, home).start()
    for h in halves:
        total = po_s[h, me_a[h]].astype(F32)
        for slot in [m[0] for m in sums] + [m[0] for m in added]:
            if slot not in half_way:
                sum_copy(h, slot, 0, 1).wait_recv()
                total = total + po_r[h, slot].astype(F32)
        mo_ref[:, cols_of[h]] = total.astype(BF16)

    for h in halves:
        wait_all(True, 8, pi, h)
        total = pi[h, 0].astype(F32)
        for p in range(1, line):
            total = total + pi[h, p].astype(F32)
        mg_ref[:, cols_of[h]] = total.astype(BF16)

    o_store.wait()
    o_send.wait()
    q_send.wait_send()
    sent_all(True, 0, ids_from, idsg)
    sent_all(True, 9, gates_from, gatesg)
    sent_all(True, 1, x_from, xg)
    sent_all(False, 3, block_of(sx), rx)
    sent_all(False, 4, block_of(sg), rg)
    sent_all(False, 5, block_of(so), bo)
    sent_all(False, 6, block_of(si), bi)
    sent_all(True, 8, block_of(pi_s), pi)
    for h in halves:
        for n in range(len(near)):
            grad_near(h, n).wait_send()
        for n in range(len(passed_on)):
            grad_pass(h, n).wait_send()
        for slot, home, offset in sums:
            sum_copy(h, slot, home, offset).wait_send()
        for slot, home, _ in added:
            sum_copy(h, slot, home, home).wait_send()

    def kv_sent(j, carry):
        @pl.when(j != g)
        def _():
            kv_copy(j, 0, k_hbm, kbuf).wait_send()
            kv_copy(j, 1, v_hbm, vbuf).wait_send()

        return carry

    lax.fori_loop(2 * chip, n_group, kv_sent, 0)


def hand_over(pieces, attn, out, grad_in, attn_o, out_o, grad_o, attn_v, out_v, grad_v, came, went):
    n = attn.shape[0] // pieces
    parts = [
        (attn.at[i * n : i * n + n], attn_v.at[i * n : i * n + n], attn_o.at[i * n : i * n + n])
        for i in range(pieces)
    ] + [(out, out_v, out_o), (grad_in, grad_v, grad_o)]
    reads = [pltpu.make_async_copy(r, v, came.at[i]) for i, (r, v, _) in enumerate(parts)]
    writes = [pltpu.make_async_copy(v, w, went.at[i]) for i, (_, v, w) in enumerate(parts)]
    for read in reads:
        read.start()
    for read, write in zip(reads, writes):
        read.wait()
        write.start()
    for write in writes:
        write.wait()


def shards(queries, keys, values, moe_x, expert_ids, gates, grad_out, w_gate, w_up, w_down):
    n_group = lax.axis_size("group")
    line = LINE
    pos, q_width = queries.shape[1:]
    tok, width = moe_x.shape[1:]
    topk = expert_ids.shape[2]
    ffe = w_gate.shape[2]
    half = q_width // 2
    n_heads = half // HD
    rows = line * CAP * line
    n_tok = line * tok
    chunk = min(CHUNK, n_group)
    vmem = pl.BlockSpec(memory_space=pltpu.VMEM)
    hbm = pl.BlockSpec(memory_space=pl.ANY)
    slots = pltpu.VMEM((2, line, CAP, line, width // 2), BF16)
    block = pltpu.VMEM((2, line, tok, width // 2), BF16)
    state = pltpu.VMEM((n_heads, 2 * pos, HD), F32)
    attn, out, grad_in = pl.pallas_call(
        functools.partial(fused, (n_group, line, tok, topk, chunk)),
        out_shape=(
            jax.ShapeDtypeStruct((pos, q_width), BF16),
            jax.ShapeDtypeStruct((tok, width), BF16),
            jax.ShapeDtypeStruct((tok, width), BF16),
        ),
        in_specs=[hbm] * 10,
        out_specs=(hbm, vmem, vmem),
        scratch_shapes=[
            pltpu.VMEM((width, ffe), BF16),
            pltpu.VMEM((width, ffe), BF16),
            pltpu.VMEM((ffe, width), BF16),
            pltpu.VMEM((2, pos, half), BF16),
            pltpu.VMEM((n_group, pos, HD), BF16),
            pltpu.VMEM((n_group, pos, HD), BF16),
            pltpu.VMEM((2, pos, half), BF16),
            state,
            state,
            state,
            pltpu.VMEM((2, line, topk, tok), jnp.int32),
            pltpu.VMEM((2, line, topk, tok), F32),
            block,
            block,
            pltpu.VMEM((2, rows, n_tok), F32),
            pltpu.VMEM((2, rows, n_tok), F32),
        ]
        + [slots] * 8
        + [block] * 4
        + [
            pltpu.SemaphoreType.DMA((2 * FAMILIES, line)),
            pltpu.SemaphoreType.DMA((2 * FAMILIES, line)),
            pltpu.SemaphoreType.DMA((2, n_group)),
            pltpu.SemaphoreType.DMA((2, n_group)),
            pltpu.SemaphoreType.DMA((2,)),
            pltpu.SemaphoreType.DMA((2,)),
            pltpu.SemaphoreType.DMA((14,)),
        ],
        compiler_params=pltpu.CompilerParams(
            collective_id=0, has_side_effects=True, vmem_limit_bytes=60 * 1024 * 1024
        ),
    )(
        moe_x[0],
        expert_ids[0].T,
        gates[0].T,
        grad_out[0],
        keys[0],
        values[0],
        queries[0],
        w_gate[0],
        w_up[0],
        w_down[0],
    )
    pieces = 4
    attn, out, grad_in = pl.pallas_call(
        functools.partial(hand_over, pieces),
        out_shape=tuple(jax.ShapeDtypeStruct(t.shape, BF16) for t in (attn, out, grad_in)),
        in_specs=[hbm] * 3,
        out_specs=(hbm,) * 3,
        scratch_shapes=[
            pltpu.VMEM(attn.shape, BF16),
            pltpu.VMEM(out.shape, BF16),
            pltpu.VMEM(out.shape, BF16),
            pltpu.SemaphoreType.DMA((pieces + 2,)),
            pltpu.SemaphoreType.DMA((pieces + 2,)),
        ],
    )(attn, out, grad_in)
    return attn[None], out[None], grad_in[None]


def solution(mesh):
    tokens = P("group", ("seq", "tp"), None)
    heads = P("seq", "group", "tp")
    weights = P(("seq", "tp"), None, None)
    return jax.shard_map(
        shards,
        mesh=mesh,
        in_specs=(heads,) * 3 + (tokens,) * 4 + (weights,) * 3,
        out_specs=(heads, tokens, tokens),
        check_vma=False,
    )
```

time: 94.9 us -> 88.6 us (0.934)
  the two profiles are of different devices: /device:TPU:14 before, /device:TPU:1 now
where the time goes in v4:
time: 88.6 us; the launch traced here: 88.5 us
  Pallas kernels  87.8 us (99%)
    pallas_call x1, Pallas kernels, shards(): pl.pallas_call(functools.partial(fused, (n_group, line, tok, topk, chunk)...  85.9 us
    pallas_call x1, Pallas kernels, shards(): pl.pallas_call(functools.partial(hand_over, pieces), out_shape=tuple((jax...  1.89 us

profile of v4, /device:TPU:1, one launch (start us, length us, event | category | flops | bytes accessed | tf_op | source)
XLA Modules:
  0.0 88.5 jit_solution(11897619641432384628)
XLA Ops:
  0.6 85.9 %shard_map.121 = (bf16[128,2048]{1,0:T(8,128)(2,1)}, bf16[16,2048]{1,0:T(8,128)(2,1)}, bf16[16,2048]{1,0:T(8,128)(2,1)}) custom-call(bf16[16,2048]{1,0:T(8,128)(2,1)} %bitcast.21, s32[8,16]{1,0:T(8,128)} %bitcast.25, f32[8,16]{1,0:T(8,128)} %bitcast.26, bf16[16,2048]{1,0:T(8,128)(2,1)} %bitcast.22, bf16[128,256]{1,0:T(8,128)(2,1)} %bitcast.23, ...), custom_call_target="tpu_custom_call" | custom-call | tf_op jit(solution)/shard_map/pallas_call | solution.py:646
  86.6 1.9 %shard_map.122 = (bf16[128,2048]{1,0:T(8,128)(2,1)}, bf16[16,2048]{1,0:T(8,128)(2,1)}, bf16[16,2048]{1,0:T(8,128)(2,1)}) custom-call(bf16[128,2048]{1,0:T(8,128)(2,1)} %get-tuple-element.9.attn, bf16[16,2048]{1,0:T(8,128)(2,1)} %get-tuple-element.10.out, bf16[16,2048]{1,0:T(8,128)(2,1)} %get-tuple-element.11.grad_in), custom_call_target="tpu_custom_call" | custom-call | tf_op jit(solution)/shard_map/pallas_call | solution.py:700
